TPU v7x, 256 devices: a whole 4x4x8 slice. The times are simulated.
256 devices in a mesh: ka: 8 (over y_lo, x), hist: 32 (over y_hi, z, core).
Axes of the slice: x: 4, y: 4 (y_hi: 2, y_lo: 2; y = y_hi * 2 + y_lo), z: 8, core: 2. Of those that a mesh axis runs over, the one named last changes fastest.
Arguments:
- step_index: int32 [1], replicated, may hold values from 33 to 128
- band_energy: float32 [128, 3, 1024], P('hist', None, 'ka'), may hold values from -1 to 3
- kernel_row: bfloat16 [128, 2, 3, 3, 1024], P('hist', None, None, None, 'ka'), may hold values from -0.5 to 0.5
- lattice_history: bfloat16 [128, 2, 3, 3, 128, 1024], P('hist', None, None, None, None, 'ka'), may hold values from -6 to 6, as said below
- diagonal_inverse: float32 [2, 3, 3, 1024], P(None, None, None, 'ka'), may hold values from -3 to 3
- multiplicity: int32 [1024], P('ka'), may hold values from 1 to 32, as said below
- state_energy: float32 [64], replicated, may hold values from -3 to 3
- connection: int32 [64, 6], replicated, may hold values from 0 to 63, as said below
- predicted_row: float32 [2, 64, 128], P(None, None, 'hist'), may hold values from -6 to 6
- pseudo_history: bfloat16 [128, 2, 64, 128], P('hist'), may hold values from -6 to 6, as said below
Outputs:
- lattice_row: bfloat16 [128, 2, 3, 3, 1024], P('hist', None, None, None, 'ka')
- local_row: float32 [2, 3, 3, 128], P(None, None, None, 'hist')
- pseudo_row: float32 [2, 64, 128], P(None, None, 'hist')
Inputs may be any that keep to these rules, and one draw needn't show every extreme that they name: `lattice_history`: the stored lattice propagators vanish where the column time j exceeds the row time m. `pseudo_history`: the stored pseudo-particle propagators vanish where the column time j exceeds the row time m. `multiplicity`: powers of two. For each flavour f, s -> connection[s, f] is an involution without fixed points; two states that flavour f links differ in that flavour's occupation, under a numbering of the states drawn from the seed.
All inputs are finite; a program needn't handle non-finite values.
Results may differ from a plain program's by a relative error of at most 0.012.
Values may be sent and summed in bfloat16 or wider, within the bound.
No kernel may reach another device: no remote copies, remote signals or barrier semaphores. Data moves between devices by JAX's collectives and lax.ppermute only.
A program may use at most 64 MiB of HBM per device.

v0:
```python
import jax
import jax.numpy as jnp
from jax import lax
from jax.experimental import pallas as pl
from jax.experimental.pallas import tpu as pltpu
from jax.sharding import PartitionSpec as P

time_step = 0.05
coupling = 0.02
F32 = jnp.float32
BF16 = jnp.bfloat16
ROWS = 80
CHUNKS = 4
HIGHEST = lax.Precision.HIGHEST


def split_high_low(x):
    high = x.astype(BF16).astype(F32)
    return high, x - high


def energy_rows(total):
    high, low = split_high_low(total)
    return jnp.concatenate([high, low, jnp.zeros((2, total.shape[1]), F32)], axis=0)


def terms_kernel(meta, kernel_row, energy, history, own, other, coeff, store, sems):
    current, position = meta[0], meta[1]
    wide = history.shape[4] // CHUNKS

    def fetch(i):
        columns = pl.ds(pl.multiple_of(i * wide, wide), wide)
        return pltpu.make_async_copy(
            history.at[:, :, :, :, columns, :], store.at[:, :, :, :, columns, :], sems.at[i]
        )

    for i in range(CHUNKS):
        fetch(i).start()
    block = kernel_row.shape[0]
    total = jnp.zeros(energy.shape[1:], F32)
    for m in range(block):
        time = position * block + m
        weight = jnp.where(time < current, jnp.where(time == 0, 0.5, 1.0), 0.0).astype(F32)
        total = total + energy[m] * jnp.where(time < current, 1.0, 0.0).astype(F32)
        for s in range(2):
            for a in range(3):
                rows = kernel_row[m, s, a].astype(F32) * weight
                for b in range(3):
                    coeff[m, s, a, b] = jnp.broadcast_to(rows[b : b + 1], (8, rows.shape[1]))
    rows_sent = energy_rows(total)
    low_half = lax.broadcasted_iota(jnp.int32, (8, 128), 0) < 4
    even_core = position % 2 == 0

    def sixteen(start, pair):
        groups = [[], []]
        for c in range(3):
            acc = {}
            for m in range(block):
                for b in range(3):
                    columns = pl.ds(pl.multiple_of(start, 16), 16)
                    re = store[m, 0, b, c, columns, :].astype(F32)
                    im = store[m, 1, b, c, columns, :].astype(F32)
                    for a in range(3):
                        kr = coeff[m, 0, a, b]
                        ki = coeff[m, 1, a, b]
                        for g in range(2):
                            hr, hi = re[8 * g : 8 * g + 8], im[8 * g : 8 * g + 8]
                            x = kr * hr - ki * hi
                            y = kr * hi + ki * hr
                            acc[0, a, g] = x if m + b == 0 else acc[0, a, g] + x
                            acc[1, a, g] = y if m + b == 0 else acc[1, a, g] + y
            for g in range(2):
                groups[g] += [acc[s, a, g] for s in range(2) for a in range(3)]
        for g in range(2):
            chip = pair + g
            evens, odds = [], []
            for u in range(9):
                p, q = groups[g][2 * u], groups[g][2 * u + 1]
                evens.append(jnp.where(low_half, p, pltpu.roll(q, 4, 0)))
                odds.append(jnp.where(low_half, pltpu.roll(p, 4, 0), q))
            evens.append(rows_sent * jnp.where(position > 2 * chip, 1.0, 0.0).astype(F32))
            odds.append(rows_sent * jnp.where(position > 2 * chip + 1, 1.0, 0.0).astype(F32))
            even = jnp.concatenate(evens, axis=0).astype(BF16)
            odd = jnp.concatenate(odds, axis=0).astype(BF16)
            own[chip] = jnp.where(even_core, even, odd)
            other[chip] = jnp.where(even_core, odd, even)

    @pl.loop(0, CHUNKS)
    def _(i):
        fetch(i).wait()

        @pl.loop(0, wide // 16)
        def _(h):
            sixteen(i * wide + h * 16, i * (wide // 8) + 2 * h)


def add_kernel(own, arrived, out):
    @pl.loop(0, own.shape[0])
    def _(i):
        x = own[i].astype(F32) + arrived[i].astype(F32)
        energies = energy_rows(x[72:75] + x[75:78])
        out[i] = jnp.concatenate([x[:72], energies], axis=0).astype(BF16)


def rows_kernel(meta, arrived, energy, inverse, multiplicity, fresh, sums):
    current, position = meta[0], meta[1]
    block = energy.shape[0]
    got = arrived[0].astype(F32)
    for i in range(1, arrived.shape[0]):
        got = got + arrived[i].astype(F32)
    later = got[72:75] + got[75:78]
    ends = []
    for m in reversed(range(block)):
        later = later + energy[m] * jnp.where(position * block + m < current, 1.0, 0.0).astype(F32)
        ends.append(later)
    angle = jnp.concatenate(
        [jnp.concatenate([ends[block - 1 - j][a : a + 1] for j in range(block)], axis=0) for a in range(3)],
        axis=0,
    ) * time_step
    column = lax.broadcasted_iota(jnp.int32, angle.shape, 0) % block + position * block
    in_range = (column <= current).astype(F32)
    free = [-jnp.sin(angle) * in_range, -jnp.cos(angle) * in_range]

    def right(s, b, c):
        r = ((c * 2 + s) * 3 + b) * block
        x = got[r : r + block]
        return x + free[s][b * block : (b + 1) * block] if b == c else x

    result = {}
    for c in range(3):
        side = {(s, b): right(s, b, c) for s in range(2) for b in range(3)}
        for a in range(3):
            re = im = 0.0
            for b in range(3):
                dr, di = inverse[0, a, b : b + 1, :], inverse[1, a, b : b + 1, :]
                re = re + dr * side[0, b] - di * side[1, b]
                im = im + dr * side[1, b] + di * side[0, b]
            result[0, a, c], result[1, a, c] = re, im
    entries = [result[s, a, c] for s in range(2) for a in range(3) for c in range(3)]
    for i, x in enumerate(entries):
        fresh[i] = x
    lanes = got.shape[1]
    entries += [jnp.ones((1, lanes), F32), jnp.zeros((lanes - 73, lanes), F32)]
    table = jnp.concatenate(entries, axis=0)
    weights = jnp.broadcast_to(multiplicity[...].astype(F32), (8, lanes))
    sums[...] = lax.dot_general(
        weights, table, (((1,), (1,)), ((), ())), precision=HIGHEST, preferred_element_type=F32
    )


VMEM = pl.BlockSpec(memory_space=pltpu.VMEM)
SMEM = pl.BlockSpec(memory_space=pltpu.SMEM)
ANY = pl.BlockSpec(memory_space=pl.ANY)


def per_device(
    step_index,
    band_energy,
    kernel_row,
    lattice_history,
    diagonal_inverse,
    multiplicity,
    state_energy,
    connection,
    predicted_row,
    pseudo_history,
):
    current = step_index[0]
    block = band_energy.shape[0]
    lanes = band_energy.shape[2]
    hist_size = lax.axis_size("hist")
    chips = hist_size // 2
    position = lax.axis_index("hist")
    meta = jnp.stack([current, position.astype(jnp.int32)])
    owned_times = position * block + jnp.arange(block, dtype=jnp.int32)
    before_now = (owned_times < current).astype(F32)
    weight = jnp.where(owned_times == 0, 0.5, 1.0).astype(F32) * before_now
    in_range = (owned_times <= current).astype(F32)
    tiles = jax.ShapeDtypeStruct((chips, ROWS, lanes), BF16)

    own, other = pl.pallas_call(
        terms_kernel,
        out_shape=(tiles, tiles),
        in_specs=[SMEM, VMEM, VMEM, ANY],
        out_specs=(VMEM, VMEM),
        scratch_shapes=[
            pltpu.VMEM((block, 2, 3, 3, 8, lanes), F32),
            pltpu.VMEM(lattice_history.shape, BF16),
            pltpu.SemaphoreType.DMA((CHUNKS,)),
        ],
        compiler_params=pltpu.CompilerParams(vmem_limit_bytes=32 << 20),
        name="terms",
    )(meta, kernel_row, band_energy, lattice_history)
    swapped = lax.ppermute(other, "hist", [(h, h ^ 1) for h in range(hist_size)])
    paired = pl.pallas_call(
        add_kernel,
        out_shape=tiles,
        in_specs=[VMEM, VMEM],
        out_specs=VMEM,
        name="add_pair",
    )(own, swapped)
    same_core = [[2 * t + c for t in range(chips)] for c in range(2)]
    arrived = lax.all_to_all(
        paired, "hist", split_axis=0, concat_axis=0, tiled=True, axis_index_groups=same_core
    )
    fresh, sums = pl.pallas_call(
        rows_kernel,
        out_shape=(
            jax.ShapeDtypeStruct((18, block, lanes), F32),
            jax.ShapeDtypeStruct((8, lanes), F32),
        ),
        in_specs=[SMEM, VMEM, VMEM, VMEM, VMEM],
        out_specs=(VMEM, VMEM),
        name="rows",
    )(meta, arrived, band_energy, diagonal_inverse, multiplicity.reshape(1, lanes))
    lattice_row = (
        jnp.transpose(fresh, (1, 0, 2)).reshape(block, 2, 3, 3, lanes).astype(BF16)
    )
    shared = lax.all_to_all(
        sums[:, None, :], "ka", split_axis=0, concat_axis=0, tiled=True
    )
    summed = jnp.sum(shared, axis=(0, 1))
    local_rows = (summed[:72] / summed[72]).reshape(2, 3, 3, block)

    diag = jnp.stack([local_rows[:, a, a, :] for a in range(3)], axis=1)
    states = connection.shape[0]
    onehot = (
        connection[:, :, None] == jnp.arange(states, dtype=jnp.int32)[None, None, :]
    ).astype(F32)
    by_orbital = onehot.reshape(states, 3, 2, states).sum(axis=2)
    reached = jnp.einsum("sat,ptm->psam", by_orbital, predicted_row, precision=HIGHEST)
    self_real = coupling * jnp.sum(diag[0][None] * reached[0] - diag[1][None] * reached[1], axis=1)
    self_imag = coupling * jnp.sum(diag[0][None] * reached[1] + diag[1][None] * reached[0], axis=1)
    wself_real = (self_real * weight[None, :]).T
    wself_imag = (self_imag * weight[None, :]).T
    hist_real = pseudo_history[:, 0].astype(F32)
    hist_imag = pseudo_history[:, 1].astype(F32)
    sum_real = jnp.sum(
        wself_real[:, :, None] * hist_real - wself_imag[:, :, None] * hist_imag, axis=0
    )
    sum_imag = jnp.sum(
        wself_real[:, :, None] * hist_imag + wself_imag[:, :, None] * hist_real, axis=0
    )
    part = jnp.stack([sum_real, sum_imag], axis=0).astype(BF16)
    part = part.reshape(2, states, hist_size, block).transpose(2, 0, 1, 3)
    shares = lax.all_to_all(part, "hist", split_axis=0, concat_axis=0, tiled=True)
    shares = shares.astype(F32).sum(axis=0)
    elapsed = (current - owned_times).astype(F32)
    spins = state_energy[:, None] * time_step * elapsed[None, :]
    free_pseudo = jnp.stack([-jnp.sin(spins), -jnp.cos(spins)], axis=0) * in_range[None, None, :]
    return (lattice_row, local_rows, free_pseudo + shares)


def solution(mesh):
    in_specs = (
        P(),
        P("hist", None, "ka"),
        P("hist", None, None, None, "ka"),
        P("hist", None, None, None, None, "ka"),
        P(None, None, None, "ka"),
        P("ka"),
        P(),
        P(),
        P(None, None, "hist"),
        P("hist", None, None, None),
    )
    out_specs = (
        P("hist", None, None, None, "ka"),
        P(None, None, None, "hist"),
        P(None, None, "hist"),
    )
    return jax.shard_map(
        per_device, mesh=mesh, in_specs=in_specs, out_specs=out_specs, check_vma=False
    )
```

profile of v0, /device:TPU:1, one launch (start us, length us, event | category | flops | bytes accessed | tf_op | source)
XLA Modules:
  0.0 70.2 jit_solution(16512564154614912116)
XLA Ops:
  1.4 0.7 %copy.44.kernel_row = bf16[4,2,3,3,128]{4,3,2,1,0:T(4,128)(2,1)S(1)} copy(bf16[4,2,3,3,128]{4,1,3,2,0:T(2,128)(2,1)} %param.12) | data formatting | bytes 36864 | tf_op args[2]
  2.1 0.7 copy.45.energy
  2.9 1.7 %copy-done.1 = bf16[4,2,3,3,128,128]{5,4,3,2,1,0:T(8,128)(2,1)S(1)} copy-done((bf16[4,2,3,3,128,128]{5,4,3,2,1,0:T(8,128)(2,1)S(1)}, bf16[4,2,3,3,128,128]{5,4,3,2,1,0:T(8,128)(2,1)}, u32[]{:S(2)}) %copy-start.1) | copy-done | bytes 2359320
  4.5 3.2 %terms.1 = (bf16[16,80,128]{2,1,0:T(8,128)(2,1)S(1)}, bf16[16,80,128]{2,1,0:T(8,128)(2,1)S(1)}) custom-call(s32[2]{0:T(128)S(1)} %pad_add_fusion.meta, bf16[4,2,3,3,128]{4,3,2,1,0:T(4,128)(2,1)S(1)} %copy.44.kernel_row, f32[4,3,128]{2,1,0:T(4,128)S(1)} %copy.45.energy, bf16[4,2,3,3,128,128]{5,4,3,2,1,0:T(8,128)(2,1)S(1)} %copy-done.1), custom_call_target="tpu_custom_call" | custom-call | tf_op jit(solution)/shard_map/terms/pallas_call | solution.py:181
  7.8 0.7 %copy-done.2 = bf16[16,80,128]{2,1,0:T(8,128)(2,1)} copy-done((bf16[16,80,128]{2,1,0:T(8,128)(2,1)}, bf16[16,80,128]{2,1,0:T(8,128)(2,1)S(1)}, u32[]{:S(2)}) %copy-start.2) | copy-done | bytes 327704
  8.5 3.2 %collective-permute-start = (bf16[16,80,128]{2,1,0:T(8,128)(2,1)S(1)}, bf16[16,80,128]{2,1,0:T(8,128)(2,1)S(1)}, u32[]{:S(2)}, u32[]{:S(2)}) collective-permute-start(bf16[16,80,128]{2,1,0:T(8,128)(2,1)S(1)} %get-tuple-element.8), channel_id=1, source_target_pairs={{0,1},{1,0},{2,3},{3,2},{4,5},{5,4},{6,7},{7,6},{8,9},{9,8},{10,11... | collective-permute-start | bytes 983048 | tf_op jit(solution)/shard_map/ppermute | solution.py:194
  11.7 1.2 %collective-permute-done.arrived = bf16[16,80,128]{2,1,0:T(8,128)(2,1)S(1)} collective-permute-done((bf16[16,80,128]{2,1,0:T(8,128)(2,1)S(1)}, bf16[16,80,128]{2,1,0:T(8,128)(2,1)S(1)}, u32[]{:S(2)}, u32[]{:S(2)}) %collective-permute-start) | collective-permute-done | bytes 327712 | tf_op jit(solution)/shard_map/ppermute | solution.py:194
  13.0 0.7 %copy-done.6 = bf16[16,80,128]{2,1,0:T(8,128)(2,1)} copy-done((bf16[16,80,128]{2,1,0:T(8,128)(2,1)}, bf16[16,80,128]{2,1,0:T(8,128)(2,1)S(1)}, u32[]{:S(2)}) %copy-start.6) | copy-done | bytes 327704
  13.7 2.0 %add_pair.1 = bf16[16,80,128]{2,1,0:T(8,128)(2,1)} custom-call(bf16[16,80,128]{2,1,0:T(8,128)(2,1)} %copy-done.2, bf16[16,80,128]{2,1,0:T(8,128)(2,1)} %copy-done.6), custom_call_target="tpu_custom_call" | custom-call | tf_op jit(solution)/shard_map/add_pair/pallas_call | solution.py:195
  15.8 9.2 %all-to-all-start = ((bf16[16,80,128]{2,1,0:T(8,128)(2,1)}), bf16[16,80,128]{2,1,0:T(8,128)(2,1)S(1)}, u32[]{:S(2)}, u32[]{:S(2)}) async-start(bf16[16,80,128]{2,1,0:T(8,128)(2,1)} %add_pair.1), calls=%async_computation | async-start | bytes 655360 | tf_op jit(solution)/shard_map/all_to_all | solution.py:203
  25.0 0.6 copy.47.inverse
  26.1 10.2 %all-to-all-done.arrived = bf16[16,80,128]{2,1,0:T(8,128)(2,1)S(1)} async-done(((bf16[16,80,128]{2,1,0:T(8,128)(2,1)}), bf16[16,80,128]{2,1,0:T(8,128)(2,1)S(1)}, u32[]{:S(2)}, u32[]{:S(2)}) %all-to-all-start) | async-done | bytes 327712 | tf_op jit(solution)/shard_map/all_to_all | solution.py:203
  36.4 0.7 %copy-done.5 = bf16[16,80,128]{2,1,0:T(8,128)(2,1)} copy-done((bf16[16,80,128]{2,1,0:T(8,128)(2,1)}, bf16[16,80,128]{2,1,0:T(8,128)(2,1)S(1)}, u32[]{:S(2)}) %copy-start.5) | copy-done | bytes 327704
  37.1 1.9 %rows.1 = (f32[18,4,128]{2,1,0:T(4,128)}, f32[8,128]{1,0:T(8,128)}) custom-call(s32[2]{0:T(128)} %copy-done.4, bf16[16,80,128]{2,1,0:T(8,128)(2,1)} %copy-done.5, f32[4,3,128]{2,1,0:T(4,128)} %copy-done.3, f32[2,3,3,128]{3,2,1,0:T(4,128)} %copy.47.inverse, s32[1,128]{1,0:T(1,128)} %bitcast.76), custom_call_target="tpu_custom_call" | custom-call | tf_op jit(solution)/shard_map/rows/pallas_call | solution.py:206
  39.0 4.1 %all-to-all-start.1 = ((f32[8,1,128]{2,1,0:T(1,128)}), f32[8,1,128]{2,1,0:T(1,128)S(1)}, u32[]{:S(2)}, u32[]{:S(2)}) async-start(f32[8,1,128]{2,1,0:T(1,128)} %bitcast.72), calls=%async_computation.1 | async-start | bytes 8192 | tf_op jit(solution)/shard_map/all_to_all | solution.py:219
  43.1 4.9 %all-to-all-done.1 = f32[8,1,128]{2,1,0:T(1,128)S(1)} async-done(((f32[8,1,128]{2,1,0:T(1,128)}), f32[8,1,128]{2,1,0:T(1,128)S(1)}, u32[]{:S(2)}, u32[]{:S(2)}) %all-to-all-start.1) | async-done | bytes 4128 | tf_op jit(solution)/shard_map/all_to_all | solution.py:219
  48.7 0.6 slice_divide_fusion
  50.1 0.7 %reshape.147 = bf16[32,2,256]{2,1,0:T(2,128)(2,1)} reshape(bf16[32,2,4,64]{3,2,1,0:T(4,128)(2,1)S(1)} %copy_bitcast_fusion.2) | data formatting | bytes 65536
  50.8 9.2 %all-to-all-start.2 = ((bf16[32,2,256]{2,1,0:T(2,128)(2,1)}), bf16[32,2,256]{2,1,0:T(2,128)(2,1)S(1)}, u32[]{:S(2)}, u32[]{:S(2)}) async-start(bf16[32,2,256]{2,1,0:T(2,128)(2,1)} %reshape.147), calls=%async_computation.2 | async-start | bytes 65536 | tf_op jit(solution)/shard_map/all_to_all | solution.py:246
  60.0 0.8 %convert_element_type.45 = bf16[18,4,128]{2,1,0:T(4,128)(2,1)S(1)} convert(f32[18,4,128]{2,1,0:T(4,128)} %get-tuple-element.9) | non-fusion elementwise | flops 9216 | bytes 55296 | tf_op jit(solution)/shard_map/convert_element_type | solution.py:217
  60.8 0.6 copy.54
  61.4 0.6 copy.55
  62.0 7.4 %all-to-all-done.2 = bf16[32,2,256]{2,1,0:T(2,128)(2,1)S(1)} async-done(((bf16[32,2,256]{2,1,0:T(2,128)(2,1)}), bf16[32,2,256]{2,1,0:T(2,128)(2,1)S(1)}, u32[]{:S(2)}, u32[]{:S(2)}) %all-to-all-start.2) | async-done | bytes 32800 | tf_op jit(solution)/shard_map/all_to_all | solution.py:246
  69.6 0.7 fusion.5
  (42 shorter events, 2.1 us)
Async XLA Ops:
  0.6 25.2 %copy-start = (f32[2,64,4]{1,2,0:T(4,128)S(1)}, f32[2,64,4]{1,2,0:T(4,128)}, u32[]{:S(2)}) copy-start(f32[2,64,4]{1,2,0:T(4,128)} %param.18) | copy-start | bytes 6148
  0.6 11.1 %copy-start.10 = (f32[64]{0:T(128)S(1)}, f32[64]{0:T(128)}, u32[]{:S(2)}) copy-start(f32[64]{0:T(128)} %param.16) | copy-start | bytes 772
  0.7 24.3 %copy-start.8 = (f32[2,3,3,128]{3,0,2,1:T(2,128)S(1)}, f32[2,3,3,128]{3,0,2,1:T(2,128)}, u32[]{:S(2)}) copy-start(f32[2,3,3,128]{3,0,2,1:T(2,128)} %param.14) | copy-start | bytes 27652
  0.7 24.9 %copy-start.9 = (s32[64,6]{0,1:T(8,128)S(1)}, s32[64,6]{0,1:T(8,128)}, u32[]{:S(2)}) copy-start(s32[64,6]{0,1:T(8,128)} %param.17) | copy-start | bytes 4612
  2.8 33.6 %copy-start.3 = (f32[4,3,128]{2,1,0:T(4,128)}, f32[4,3,128]{2,1,0:T(4,128)S(1)}, u32[]{:S(2)}) copy-start(f32[4,3,128]{2,1,0:T(4,128)S(1)} %copy.45.energy) | copy-start | bytes 18436
  2.9 1.7 %copy-start.1 = (bf16[4,2,3,3,128,128]{5,4,3,2,1,0:T(8,128)(2,1)S(1)}, bf16[4,2,3,3,128,128]{5,4,3,2,1,0:T(8,128)(2,1)}, u32[]{:S(2)}) copy-start(bf16[4,2,3,3,128,128]{5,4,3,2,1,0:T(8,128)(2,1)} %history.1) | copy-start | bytes 7077892
  4.5 31.8 %copy-start.4 = (s32[2]{0:T(128)}, s32[2]{0:T(128)S(1)}, u32[]{:S(2)}) copy-start(s32[2]{0:T(128)S(1)} %pad_add_fusion.meta) | copy-start | bytes 28
  4.5 45.1 %copy-start.7 = (bf16[4,2,64,128]{3,2,1,0:T(8,128)(2,1)S(1)}, bf16[4,2,64,128]{3,2,1,0:T(8,128)(2,1)}, u32[]{:S(2)}) copy-start(bf16[4,2,64,128]{3,2,1,0:T(8,128)(2,1)} %param.19) | copy-start | bytes 393220
  7.8 0.7 %copy-start.2 = (bf16[16,80,128]{2,1,0:T(8,128)(2,1)}, bf16[16,80,128]{2,1,0:T(8,128)(2,1)S(1)}, u32[]{:S(2)}) copy-start(bf16[16,80,128]{2,1,0:T(8,128)(2,1)S(1)} %get-tuple-element.7.own) | copy-start | bytes 983044
  8.5 4.5 %collective-permute-start = (bf16[16,80,128]{2,1,0:T(8,128)(2,1)S(1)}, bf16[16,80,128]{2,1,0:T(8,128)(2,1)S(1)}, u32[]{:S(2)}, u32[]{:S(2)}) collective-permute-start(bf16[16,80,128]{2,1,0:T(8,128)(2,1)S(1)} %get-tuple-element.8), channel_id=1, source_target_pairs={{0,1},{1,0},{2,3},{3,2},{4,5},{5,4},{6,7},{7,6},{8,9},{9,8},{10,11... | collective-permute-start | bytes 983048 | tf_op jit(solution)/shard_map/ppermute | solution.py:194
  13.0 0.7 %copy-start.6 = (bf16[16,80,128]{2,1,0:T(8,128)(2,1)}, bf16[16,80,128]{2,1,0:T(8,128)(2,1)S(1)}, u32[]{:S(2)}) copy-start(bf16[16,80,128]{2,1,0:T(8,128)(2,1)S(1)} %collective-permute-done.arrived) | copy-start | bytes 983044
  15.8 20.6 %all-to-all-start = ((bf16[16,80,128]{2,1,0:T(8,128)(2,1)}), bf16[16,80,128]{2,1,0:T(8,128)(2,1)S(1)}, u32[]{:S(2)}, u32[]{:S(2)}) async-start(bf16[16,80,128]{2,1,0:T(8,128)(2,1)} %add_pair.1), calls=%async_computation | async-start | bytes 655360 | tf_op jit(solution)/shard_map/all_to_all | solution.py:203
  36.4 0.7 %copy-start.5 = (bf16[16,80,128]{2,1,0:T(8,128)(2,1)}, bf16[16,80,128]{2,1,0:T(8,128)(2,1)S(1)}, u32[]{:S(2)}) copy-start(bf16[16,80,128]{2,1,0:T(8,128)(2,1)S(1)} %all-to-all-done.arrived) | copy-start | bytes 983044
  39.0 9.1 %all-to-all-start.1 = ((f32[8,1,128]{2,1,0:T(1,128)}), f32[8,1,128]{2,1,0:T(1,128)S(1)}, u32[]{:S(2)}, u32[]{:S(2)}) async-start(f32[8,1,128]{2,1,0:T(1,128)} %bitcast.72), calls=%async_computation.1 | async-start | bytes 8192 | tf_op jit(solution)/shard_map/all_to_all | solution.py:219
  50.8 18.6 %all-to-all-start.2 = ((bf16[32,2,256]{2,1,0:T(2,128)(2,1)}), bf16[32,2,256]{2,1,0:T(2,128)(2,1)S(1)}, u32[]{:S(2)}, u32[]{:S(2)}) async-start(bf16[32,2,256]{2,1,0:T(2,128)(2,1)} %reshape.147), calls=%async_computation.2 | async-start | bytes 65536 | tf_op jit(solution)/shard_map/all_to_all | solution.py:246
where the time goes:
time: 70.8 us; the launch traced here: 70.2 us
  starting transfers between devices  25.7 us (36%)
  waiting for transfers between devices  23.8 us (34%)
  local copies, waits for them, and re-layouts  8.91 us (13%)
  Pallas kernels  7.14 us (10%)
  other arithmetic  2.84 us (4%)
  between operations  1.5 us (2%)
    all_to_all x1, waiting for transfers between devices, per_device(): lax.all_to_all(paired, 'hist', split_axis=0, concat_axis=0, tiled=True, a...  10.2 us
    all_to_all x1, starting transfers between devices, per_device(): lax.all_to_all(paired, 'hist', split_axis=0, concat_axis=0, tiled=True, a...  9.18 us
    all_to_all x1, starting transfers between devices, per_device(): lax.all_to_all(part, 'hist', split_axis=0, concat_axis=0, tiled=True)  9.18 us
    unnamed x30, local copies, waits for them, and re-layouts  7.99 us
    all_to_all x1, waiting for transfers between devices, per_device(): lax.all_to_all(part, 'hist', split_axis=0, concat_axis=0, tiled=True)  7.42 us
    all_to_all x1, waiting for transfers between devices, per_device(): lax.all_to_all(sums[:, None, :], 'ka', split_axis=0, concat_axis=0, tiled...  4.92 us
    all_to_all x1, starting transfers between devices, per_device(): lax.all_to_all(sums[:, None, :], 'ka', split_axis=0, concat_axis=0, tiled...  4.13 us
    ppermute x1, starting transfers between devices, per_device(): lax.ppermute(other, 'hist', [(h, h ^ 1) for h in range(hist_size)])  3.24 us
  transfers between devices with their start and end apart: 4, of which 4 were waited for; matrix products, arithmetic and copies ran while one was open for 4% of the time, Pallas kernels for 0%

commit v1 on v0

v1 whole, which is shorter than its diff:
```python
import jax
import jax.numpy as jnp
from jax import lax
from jax.experimental import pallas as pl
from jax.experimental.pallas import tpu as pltpu
from jax.sharding import PartitionSpec as P

time_step = 0.05
coupling = 0.02
F32 = jnp.float32
BF16 = jnp.bfloat16
HIGHEST = lax.Precision.HIGHEST
TERMS = 80
INPUTS = 24
CHUNKS = 4


def flag(condition):
    return jnp.where(condition, 1.0, 0.0).astype(F32)


def low_half(lanes=128):
    return lax.broadcasted_iota(jnp.int32, (8, lanes), 0) < 4


def high_low(x):
    high = x.astype(BF16).astype(F32)
    return jnp.where(low_half(x.shape[1]), high, x - high)


def interleave(p, q):
    low = low_half(p.shape[1])
    return jnp.where(low, p, pltpu.roll(q, 4, 0)), jnp.where(low, pltpu.roll(p, 4, 0), q)


def terms_kernel(step, kernel_row, energy, predicted, pseudo, history, own, other, coeff, turned, store, sems):
    current, position = step[0], lax.axis_index("hist")
    wide = history.shape[4] // CHUNKS

    def fetch(i):
        columns = pl.ds(pl.multiple_of(i * wide, wide), wide)
        return pltpu.make_async_copy(
            history.at[:, :, :, :, columns, :], store.at[:, :, :, :, columns, :], sems.at[i]
        )

    for i in range(CHUNKS):
        fetch(i).start()
    block = energy.shape[1]
    lanes = energy.shape[2]
    zero = jnp.zeros((1, lanes), F32)
    total = jnp.zeros((3, lanes), F32)
    for m in range(block):
        time = position * block + m
        weight = jnp.where(time < current, jnp.where(time == 0, 0.5, 1.0), 0.0).astype(F32)
        total = total + energy[:, m, :] * flag(time < current)
        for a in range(3):
            for b in range(3):
                rows = kernel_row[m, a, b].astype(F32) * weight
                for s in range(2):
                    coeff[m, s, a, b] = jnp.broadcast_to(rows[s : s + 1], (8, lanes))
        both = jnp.concatenate([pseudo[m, 0], pseudo[m, 1]], axis=0).astype(F32)
        turned[m] = both.T
    energies = high_low(jnp.concatenate([total, zero, total, zero], axis=0))
    ahead = jnp.concatenate([predicted[0], predicted[1]], axis=1)
    ahead = high_low(jnp.concatenate([ahead, ahead], axis=0))
    even_core = position % 2 == 0

    def sixteen(start, pair):
        groups = [[], []]
        for c in range(3):
            acc = {}
            for m in range(block):
                for b in range(3):
                    columns = pl.ds(pl.multiple_of(start, 16), 16)
                    re = store[m, 0, b, c, columns, :].astype(F32)
                    im = store[m, 1, b, c, columns, :].astype(F32)
                    for a in range(3):
                        kr = coeff[m, 0, a, b]
                        ki = coeff[m, 1, a, b]
                        for g in range(2):
                            hr, hi = re[8 * g : 8 * g + 8], im[8 * g : 8 * g + 8]
                            x = kr * hr - ki * hi
                            y = kr * hi + ki * hr
                            acc[0, a, g] = x if m + b == 0 else acc[0, a, g] + x
                            acc[1, a, g] = y if m + b == 0 else acc[1, a, g] + y
            for g in range(2):
                groups[g] += [acc[s, a, g] for s in range(2) for a in range(3)]
        for g in range(2):
            chip = pair + g
            evens, odds = [], []

            def add(p, q):
                x, y = interleave(p, q)
                evens.append(x)
                odds.append(y)

            for u in range(9):
                add(groups[g][2 * u], groups[g][2 * u + 1])
            evens.append(energies * flag(position > 2 * chip))
            odds.append(energies * flag(position > 2 * chip + 1))
            columns = pl.ds(pl.multiple_of(start + 8 * g, 8), 8)
            for m in range(0, block, 2):
                add(turned[m, columns, :], turned[m + 1, columns, :])
            evens.append(ahead)
            odds.append(ahead)
            even = jnp.concatenate(evens, axis=0).astype(BF16)
            odd = jnp.concatenate(odds, axis=0).astype(BF16)
            own[chip] = jnp.where(even_core, even, odd)
            other[chip] = jnp.where(even_core, odd, even)

    @pl.loop(0, CHUNKS)
    def _(i):
        fetch(i).wait()

        @pl.loop(0, wide // 16)
        def _(h):
            sixteen(i * wide + h * 16, i * (wide // 8) + 2 * h)


def add_kernel(own, arrived, out):
    @pl.loop(0, own.shape[0] // 4)
    def _(i):
        for u in range(4):
            t = 4 * i + u
            x = own[t, :TERMS].astype(F32) + arrived[t, :TERMS].astype(F32)
            energies = x[72:80]
            energies = high_low(energies + pltpu.roll(energies, 4, 0))
            out[t, :TERMS] = jnp.concatenate([x[:72], energies], axis=0).astype(BF16)
            out[t, TERMS : TERMS + INPUTS] = own[t, TERMS:]
            out[t, TERMS + INPUTS :] = arrived[t, TERMS:]


def rows_kernel(step, arrived, energy, inverse, multiplicity, fresh, sums):
    current, position = step[0], lax.axis_index("hist")
    block = energy.shape[1]
    lanes = energy.shape[2]
    got = arrived[0, :TERMS].astype(F32)
    for i in range(1, arrived.shape[0]):
        got = got + arrived[i, :TERMS].astype(F32)
    later = got[72:75] + got[76:79]
    ends = []
    for m in reversed(range(block)):
        later = later + energy[:, m, :] * flag(position * block + m < current)
        ends.append(later)
    angle = jnp.concatenate(
        [ends[block - 1 - j][a : a + 1] for a in range(3) for j in range(block)], axis=0
    )
    angle = angle * time_step
    column = lax.broadcasted_iota(jnp.int32, angle.shape, 0) % block + position * block
    in_range = (column <= current).astype(F32)
    free = [-jnp.sin(angle) * in_range, -jnp.cos(angle) * in_range]

    def right(s, b, c):
        r = ((c * 2 + s) * 3 + b) * block
        x = got[r : r + block]
        return x + free[s][b * block : (b + 1) * block] if b == c else x

    entries = {}
    for c in range(3):
        side = {(s, b): right(s, b, c) for s in range(2) for b in range(3)}
        for a in range(3):
            re = im = 0.0
            for b in range(3):
                dr, di = inverse[a, b, 0:1, :], inverse[a, b, 1:2, :]
                re = re + dr * side[0, b] - di * side[1, b]
                im = im + dr * side[1, b] + di * side[0, b]
            entries[a, c, 0], entries[a, c, 1] = re, im
    entries = [entries[a, c, s] for a in range(3) for c in range(3) for s in range(2)]
    for i, x in enumerate(entries):
        fresh[i] = x
    entries += [jnp.ones((1, lanes), F32), jnp.zeros((lanes - 73, lanes), F32)]
    table = jnp.concatenate(entries, axis=0)
    weights = jnp.broadcast_to(multiplicity[...].astype(F32), (8, lanes))
    message = lax.dot_general(
        weights, table, (((1,), (1,)), ((), ())), precision=HIGHEST, preferred_element_type=F32
    )
    for i in range(0, sums.shape[0], 8):
        sums[i : i + 8] = message


def signed_swap(x):
    lanes = x.shape[1]
    swapped = pltpu.roll(x, lanes // 2, 1)
    lower = lax.broadcasted_iota(jnp.int32, x.shape, 1) < lanes // 2
    return jnp.where(lower, -swapped, swapped)


def prepare_kernel(step, arrived, links, levels, fresh, product, free, lattice, high, low, raw, reached):
    current, position = step[0], lax.axis_index("hist")
    chips = arrived.shape[0]
    states = links.shape[1]
    block = fresh.shape[1]
    even_core = position % 2 == 0

    @pl.loop(0, chips)
    def _(t):
        mine = arrived[t, TERMS : TERMS + INPUTS].astype(F32)
        near = arrived[t, TERMS + INPUTS :].astype(F32)
        even = jnp.where(even_core, mine, near)
        odd = jnp.where(even_core, near, mine)
        raw[2 * t] = even[:16]
        raw[2 * t + 1] = odd[:16]
        times = pl.ds(pl.multiple_of(8 * t, 8), 8)
        high[times, :], low[times, :] = interleave(even[16:], odd[16:])

    state = lax.broadcasted_iota(jnp.int32, (states, states), 0)
    for a in range(3):
        link = flag(links[2 * a : 2 * a + 1, :] == state) + flag(links[2 * a + 1 : 2 * a + 2, :] == state)
        link = jnp.concatenate([link, link], axis=1).astype(BF16)
        for p in range(2):
            half = slice(p * states, (p + 1) * states)
            part = jnp.dot(high[:, half].astype(BF16), link, preferred_element_type=F32)
            part = part + jnp.dot(low[:, half].astype(BF16), link, preferred_element_type=F32)
            reached[a, p] = part

    @pl.loop(0, chips)
    def _(t):
        times = pl.ds(pl.multiple_of(8 * t, 8), 8)
        time = lax.broadcasted_iota(jnp.int32, (8, 2 * states), 0) + 8 * t
        weight = jnp.where(time < current, jnp.where(time == 0, 0.5, 1.0), 0.0) * coupling
        for j in range(block):
            first = raw[2 * t, pl.ds(j, 4, stride=4), :]
            second = raw[2 * t + 1, pl.ds(j, 4, stride=4), :]
            past = jnp.concatenate([first, second], axis=0) * weight.astype(F32)
            for a in range(3):
                x = reached[a, 0, times, :] * past
                y = reached[a, 1, times, :] * past
                product[a, j, times, :] = x + signed_swap(y)

    column = lax.broadcasted_iota(jnp.int32, (block, 2 * states), 0) + position * block
    elapsed = (current - column).astype(F32)
    level = jnp.concatenate([levels[...], levels[...]], axis=1)
    spin = level * time_step * elapsed
    lower = lax.broadcasted_iota(jnp.int32, spin.shape, 1) < states
    free[...] = jnp.where(lower, -jnp.sin(spin), -jnp.cos(spin)) * (column <= current).astype(F32)
    for a in range(3):
        for c in range(3):
            i = (a * 3 + c) * 2
            re, im = fresh[i], fresh[i + 1]
            for j in range(block):
                pair = jnp.concatenate([re[j : j + 1], im[j : j + 1]], axis=0)
                lattice[j, a, c] = pair.astype(BF16)


def finish_kernel(got, product, free, local, pseudo, rows):
    position = lax.axis_index("hist")
    size = rows.shape[0]
    total = got[0:size]
    for i in range(1, got.shape[0] // size):
        total = total + got[i * size : (i + 1) * size]
    scaled = total / total[:, 72:73]
    rows[...] = scaled
    mine = rows[pl.ds(position, 1), :]
    for a in range(3):
        for c in range(3):
            i = (a * 3 + c) * 8
            local[a, c] = jnp.concatenate([mine[:, i : i + 4], mine[:, i + 4 : i + 8]], axis=0)
    block = free.shape[0]
    lane = lax.broadcasted_iota(jnp.int32, (8, 128), 1)
    row = lax.broadcasted_iota(jnp.int32, (8, 128), 0) % 4
    low = low_half()
    real = [0.0] * block
    imag = [0.0] * block
    for t in range(size // 2):
        both = jnp.where(low, scaled[2 * t : 2 * t + 1], scaled[2 * t + 1 : 2 * t + 2])
        for a in range(3):
            re = jnp.sum(jnp.where(lane == row + 32 * a, both, 0.0), axis=1, keepdims=True)
            im = jnp.sum(jnp.where(lane == row + 32 * a + 4, both, 0.0), axis=1, keepdims=True)
            for j in range(block):
                x = product[a, j, 8 * t : 8 * t + 8, :]
                real[j] = real[j] + re * x
                imag[j] = imag[j] + im * x
    real = jnp.concatenate([jnp.sum(x, axis=0, keepdims=True) for x in real], axis=0)
    imag = jnp.concatenate([jnp.sum(x, axis=0, keepdims=True) for x in imag], axis=0)
    out = free[...] + real + signed_swap(imag)
    states = out.shape[1] // 2
    pseudo[0] = out[:, :states]
    pseudo[1] = out[:, states:]


VMEM = pl.BlockSpec(memory_space=pltpu.VMEM)
SMEM = pl.BlockSpec(memory_space=pltpu.SMEM)
HBM = pl.BlockSpec(memory_space=pltpu.HBM)


def grant(mib):
    return pltpu.CompilerParams(vmem_limit_bytes=mib << 20)


def per_device(
    step_index,
    band_energy,
    kernel_row,
    lattice_history,
    diagonal_inverse,
    multiplicity,
    state_energy,
    connection,
    predicted_row,
    pseudo_history,
):
    block, _, lanes = band_energy.shape
    states, flavours = connection.shape
    ka_size, hist_size = lax.axis_size("ka"), lax.axis_size("hist")
    chips = hist_size // 2
    everyone = ka_size * hist_size
    energy = jnp.transpose(band_energy, (1, 0, 2))
    sent = jax.ShapeDtypeStruct((chips, TERMS + INPUTS, lanes), BF16)

    own, other = pl.pallas_call(
        terms_kernel,
        out_shape=(sent, sent),
        in_specs=[SMEM, VMEM, VMEM, VMEM, VMEM, HBM],
        out_specs=(VMEM, VMEM),
        scratch_shapes=[
            pltpu.VMEM((block, 2, 3, 3, 8, lanes), F32),
            pltpu.VMEM((block, block * hist_size, 2 * states), F32),
            pltpu.VMEM(lattice_history.shape, BF16),
            pltpu.SemaphoreType.DMA((CHUNKS,)),
        ],
        compiler_params=grant(16),
        name="terms",
    )(
        step_index,
        jnp.transpose(kernel_row, (0, 2, 3, 1, 4)),
        energy,
        jnp.transpose(predicted_row, (0, 2, 1)),
        pseudo_history,
        lattice_history,
    )
    swapped = lax.ppermute(other, "hist", [(h, h ^ 1) for h in range(hist_size)])
    paired = pl.pallas_call(
        add_kernel,
        out_shape=jax.ShapeDtypeStruct((chips, TERMS + 2 * INPUTS, lanes), BF16),
        in_specs=[VMEM, VMEM],
        out_specs=VMEM,
        compiler_params=grant(8),
        name="add_pair",
    )(own, swapped)
    same_core = [[2 * t + c for t in range(chips)] for c in range(2)]
    arrived = lax.all_to_all(
        paired, "hist", split_axis=0, concat_axis=0, tiled=True, axis_index_groups=same_core
    )
    fresh, sums = pl.pallas_call(
        rows_kernel,
        out_shape=(
            jax.ShapeDtypeStruct((18, block, lanes), F32),
            jax.ShapeDtypeStruct((everyone, lanes), F32),
        ),
        in_specs=[SMEM, VMEM, VMEM, VMEM, VMEM],
        out_specs=(VMEM, VMEM),
        compiler_params=grant(8),
        name="rows",
    )(
        step_index,
        arrived,
        energy,
        jnp.transpose(diagonal_inverse, (1, 2, 0, 3)),
        multiplicity.reshape(1, lanes),
    )
    shared = lax.all_to_all(
        sums.reshape(everyone, 1, lanes), ("ka", "hist"), split_axis=0, concat_axis=0, tiled=True
    )
    product, free, lattice = pl.pallas_call(
        prepare_kernel,
        out_shape=(
            jax.ShapeDtypeStruct((3, block, block * hist_size, 2 * states), F32),
            jax.ShapeDtypeStruct((block, 2 * states), F32),
            jax.ShapeDtypeStruct((block, 3, 3, 2, lanes), BF16),
        ),
        in_specs=[SMEM, VMEM, VMEM, VMEM, VMEM],
        out_specs=(VMEM, VMEM, VMEM),
        scratch_shapes=[
            pltpu.VMEM((block * hist_size, 2 * states), F32),
            pltpu.VMEM((block * hist_size, 2 * states), F32),
            pltpu.VMEM((hist_size, 16, 2 * states), F32),
            pltpu.VMEM((3, 2, block * hist_size, 2 * states), F32),
        ],
        compiler_params=grant(8),
        cost_estimate=pl.CostEstimate(flops=40_000_000, bytes_accessed=2_000_000, transcendentals=2048),
        name="prepare",
    )(step_index, arrived, connection.T, state_energy.reshape(1, states), fresh)
    local, pseudo = pl.pallas_call(
        finish_kernel,
        out_shape=(
            jax.ShapeDtypeStruct((3, 3, 2, block), F32),
            jax.ShapeDtypeStruct((2, block, states), F32),
        ),
        in_specs=[VMEM, VMEM, VMEM],
        out_specs=(VMEM, VMEM),
        scratch_shapes=[pltpu.VMEM((hist_size, lanes), F32)],
        compiler_params=grant(8),
        name="finish",
    )(shared.reshape(everyone, lanes), product, free)
    return (
        jnp.transpose(lattice, (0, 3, 1, 2, 4)),
        jnp.transpose(local, (2, 0, 1, 3)),
        jnp.transpose(pseudo, (0, 2, 1)),
    )


def solution(mesh):
    in_specs = (
        P(),
        P("hist", None, "ka"),
        P("hist", None, None, None, "ka"),
        P("hist", None, None, None, None, "ka"),
        P(None, None, None, "ka"),
        P("ka"),
        P(),
        P(),
        P(None, None, "hist"),
        P("hist", None, None, None),
    )
    out_specs = (
        P("hist", None, None, None, "ka"),
        P(None, None, None, "hist"),
        P(None, None, "hist"),
    )
    return jax.shard_map(
        per_device, mesh=mesh, in_specs=in_specs, out_specs=out_specs, check_vma=False
    )
```

time: 70.8 us -> 63.6 us (0.90)
  blocking collectives: 0 us -> 24.1 us
  waiting for transfers between devices: 23.8 us -> 11.7 us
  starting transfers between devices: 25.7 us -> 13.9 us
  local copies, waits for them, and re-layouts: 8.91 us -> 4.68 us
  other arithmetic: 2.84 us -> 0 us
    all_to_all x0 -> x1, blocking collectives: none -> 24.1 us  [per_device(): lax.all_to_all(paired, 'hist', split_axis=0, concat_axis=0, tiled=True, a...]
    all_to_all x3 -> x1, waiting for transfers between devices: 22.6 us -> 10.3 us  [per_device(): lax.all_to_all(sums.reshape(everyone, 1, lanes), ('ka', 'hist'), split_ax...]
    all_to_all x3 -> x1, starting transfers between devices: 22.5 us -> 10.6 us  [per_device(): lax.all_to_all(sums.reshape(everyone, 1, lanes), ('ka', 'hist'), split_ax...]
    unnamed x30 -> x18, local copies, waits for them, and re-layouts: 7.99 us -> 4.68 us
    pallas_call x2 -> x4, Pallas kernels: 5.25 us -> 6.66 us  [the longest x1 3.07 us: per_device(): pl.pallas_call(terms_kernel, out_shape=(sent, sent), in_specs=[SMEM, VMEM...]
    pallas_call x1, Pallas kernels: 1.88 us -> 0.96 us  [per_device(): pl.pallas_call(rows_kernel, out_shape=(jax.ShapeDtypeStruct((18, block, l...]
    convert_element_type x3 -> x0, other arithmetic: 0.79 us -> none  [the longest x1 0.78 us: per_device(): jnp.transpose(fresh, (1, 0, 2)).reshape(block, 2, 3, 3, lanes).astype(BF16)]
  transfers between devices with their start and end apart: 4 -> 2, of which waited for: 4 -> 2; matrix products, arithmetic and copies ran while one was open for 4% -> 0% of each run, Pallas kernels for 0% -> 4%
where the time goes in v1:
time: 63.6 us; the launch traced here: 63.3 us
  blocking collectives  24.1 us (38%)
  starting transfers between devices  13.9 us (22%)
  waiting for transfers between devices  11.7 us (18%)
  Pallas kernels  7.63 us (12%)
  local copies, waits for them, and re-layouts  4.68 us (7%)
  between operations  1.34 us (2%)
    all_to_all x1, blocking collectives, per_device(): lax.all_to_all(paired, 'hist', split_axis=0, concat_axis=0, tiled=True, a...  24.1 us
    all_to_all x1, starting transfers between devices, per_device(): lax.all_to_all(sums.reshape(everyone, 1, lanes), ('ka', 'hist'), split_ax...  10.6 us
    all_to_all x1, waiting for transfers between devices, per_device(): lax.all_to_all(sums.reshape(everyone, 1, lanes), ('ka', 'hist'), split_ax...  10.3 us
    unnamed x18, local copies, waits for them, and re-layouts  4.68 us
    ppermute x1, starting transfers between devices, per_device(): lax.ppermute(other, 'hist', [(h, h ^ 1) for h in range(hist_size)])  3.33 us
    pallas_call x1, Pallas kernels, per_device(): pl.pallas_call(terms_kernel, out_shape=(sent, sent), in_specs=[SMEM, VMEM...  3.07 us
    pallas_call x1, Pallas kernels, per_device(): pl.pallas_call(prepare_kernel, out_shape=(jax.ShapeDtypeStruct((3, block,...  2.49 us
    ppermute x1, waiting for transfers between devices, per_device(): lax.ppermute(other, 'hist', [(h, h ^ 1) for h in range(hist_size)])  1.4 us
  transfers between devices with their start and end apart: 2, of which 2 were waited for; matrix products, arithmetic and copies ran while one was open for 0% of the time, Pallas kernels for 4%

profile of v1, /device:TPU:1, one launch (start us, length us, event | category | flops | bytes accessed | tf_op | source)
XLA Modules:
  0.0 63.3 jit_solution(8317809879262208127)
XLA Ops:
  1.3 0.0 copy-start
  1.3 1.7 %copy-done = bf16[4,2,3,3,128,128]{5,4,3,2,1,0:T(8,128)(2,1)S(1)} copy-done((bf16[4,2,3,3,128,128]{5,4,3,2,1,0:T(8,128)(2,1)S(1)}, bf16[4,2,3,3,128,128]{5,4,3,2,1,0:T(8,128)(2,1)}, u32[]{:S(2)}) %copy-start) | copy-done | bytes 2359320
  2.9 0.9 %copy-done.1 = bf16[4,2,64,128]{3,2,1,0:T(8,128)(2,1)S(1)} copy-done((bf16[4,2,64,128]{3,2,1,0:T(8,128)(2,1)S(1)}, bf16[4,2,64,128]{3,2,1,0:T(8,128)(2,1)}, u32[]{:S(2)}) %copy-start.1) | copy-done | bytes 131096
  3.9 0.0 copy-start.2
  3.9 0.7 %copy-done.2 = f32[4,3,128]{2,0,1:T(4,128)S(1)} copy-done((f32[4,3,128]{2,0,1:T(4,128)S(1)}, f32[4,3,128]{2,0,1:T(4,128)}, u32[]{:S(2)}) %copy-start.2) | copy-done | bytes 6168
  4.5 0.0 copy-start.3
  4.5 0.7 %copy-done.3 = bf16[4,2,3,3,128]{4,1,3,2,0:T(2,128)(2,1)S(1)} copy-done((bf16[4,2,3,3,128]{4,1,3,2,0:T(2,128)(2,1)S(1)}, bf16[4,2,3,3,128]{4,1,3,2,0:T(2,128)(2,1)}, u32[]{:S(2)}) %copy-start.3) | copy-done | bytes 18456
  5.3 0.0 copy-start.5
  5.3 0.7 %copy-done.5 = f32[2,64,4]{1,2,0:T(4,128)S(1)} copy-done((f32[2,64,4]{1,2,0:T(4,128)S(1)}, f32[2,64,4]{1,2,0:T(4,128)}, u32[]{:S(2)}) %copy-start.5) | copy-done | bytes 2072
  6.0 0.0 copy-start.4
  6.0 3.1 %terms.1 = (bf16[16,104,128]{2,1,0:T(8,128)(2,1)S(1)}, bf16[16,104,128]{2,1,0:T(8,128)(2,1)S(1)}) custom-call(s32[1]{0:T(128)S(6)} %copy.14.step, bf16[4,3,3,2,128]{4,3,2,1,0:T(2,128)(2,1)S(1)} %bitcast.17, f32[3,4,128]{2,1,0:T(4,128)S(1)} %bitcast.15, f32[2,4,64]{2,1,0:T(4,128)S(1)} %bitcast.19, bf16[4,2,64,128]{3,2,1,0:T(8,128)(2,1)S(1)} %copy-done.1, ...), custom_call_target="tpu_custom_call" | custom-call | tf_op jit(solution)/shard_map/terms/pallas_call | solution.py:310
  9.0 3.3 %collective-permute-start = (bf16[16,104,128]{2,1,0:T(8,128)(2,1)S(1)}, bf16[16,104,128]{2,1,0:T(8,128)(2,1)S(1)}, u32[]{:S(2)}, u32[]{:S(2)}) collective-permute-start(bf16[16,104,128]{2,1,0:T(8,128)(2,1)S(1)} %get-tuple-element.13), channel_id=1, source_target_pairs={{0,1},{1,0},{2,3},{3,2},{4,5},{5,4},{6,7},{7,6},{8,9},{9,8},{10,11... | collective-permute-start | bytes 1277960 | tf_op jit(solution)/shard_map/ppermute | solution.py:331
  12.4 1.4 %collective-permute-done.arrived = bf16[16,104,128]{2,1,0:T(8,128)(2,1)S(1)} collective-permute-done((bf16[16,104,128]{2,1,0:T(8,128)(2,1)S(1)}, bf16[16,104,128]{2,1,0:T(8,128)(2,1)S(1)}, u32[]{:S(2)}, u32[]{:S(2)}) %collective-permute-start) | collective-permute-done | bytes 426016 | tf_op jit(solution)/shard_map/ppermute | solution.py:331
  13.8 0.1 add_pair.1
  13.9 24.1 %all_to_all.10.arrived = bf16[16,128,128]{2,1,0:T(8,128)(2,1)S(1)} all-to-all(bf16[16,128,128]{2,1,0:T(8,128)(2,1)S(1)} %add_pair.1), channel_id=1, replica_groups={{0,2,4,6,8,10,12,14,16,18,20,22,24,26,28,30},{1,3,5,7,9,11,13,15,17,19,..., dimensions={0} | all-to-all | bytes 1048576 | tf_op jit(solution)/shard_map/all_to_all | solution.py:341
  38.0 0.0 copy-done.4
  38.0 0.0 copy-done.7
  38.0 1.0 %rows.1 = (f32[18,4,128]{2,1,0:T(4,128)S(1)}, f32[256,128]{1,0:T(8,128)}) custom-call(s32[1]{0:T(128)S(6)} %copy.14.step, bf16[16,128,128]{2,1,0:T(8,128)(2,1)S(1)} %all_to_all.10.arrived, f32[3,4,128]{2,1,0:T(4,128)S(1)} %bitcast.16, f32[3,3,2,128]{3,2,1,0:T(2,128)S(1)} %bitcast.18, s32[1,128]{1,0:T(1,128)S(1)} %bitcast.21), custom_call_target="tpu_custom_call" | custom-call | tf_op jit(solution)/shard_map/rows/pallas_call | solution.py:344
  38.9 10.6 %all-to-all-start.1 = ((f32[256,1,128]{2,1,0:T(1,128)}), f32[256,1,128]{2,1,0:T(1,128)S(1)}, u32[]{:S(2)}, u32[]{:S(2)}) async-start(f32[256,1,128]{2,1,0:T(1,128)} %bitcast.9), calls=%async_computation.1 | async-start | bytes 262144 | tf_op jit(solution)/shard_map/all_to_all | solution.py:361
  49.5 0.0 copy-done.6
  49.5 0.0 copy-done.8
  49.5 2.5 %prepare.1 = (f32[3,4,128,128]{3,2,1,0:T(8,128)S(1)}, f32[4,128]{1,0:T(4,128)S(1)}, bf16[4,3,3,2,128]{4,3,2,1,0:T(2,128)(2,1)}) custom-call(s32[1]{0:T(128)S(6)} %copy.14.step, bf16[16,128,128]{2,1,0:T(8,128)(2,1)S(1)} %all_to_all.10.arrived, s32[6,64]{1,0:T(8,128)S(1)} %bitcast.20, f32[1,64]{1,0:T(1,128)S(1)} %bitcast.22, ...), custom_call_target="tpu_custom_call" | custom-call | flops 40000000 | bytes 2000000 | tf_op jit(solution)/shard_map/prepare/pallas_call | solution.py:364
  52.0 10.3 %all-to-all-done.1 = f32[256,1,128]{2,1,0:T(1,128)S(1)} async-done(((f32[256,1,128]{2,1,0:T(1,128)}), f32[256,1,128]{2,1,0:T(1,128)S(1)}, u32[]{:S(2)}, u32[]{:S(2)}) %all-to-all-start.1) | async-done | bytes 131104 | tf_op jit(solution)/shard_map/all_to_all | solution.py:361
  62.3 1.0 %finish.1 = (f32[3,3,2,4]{3,2,1,0:T(2,128)}, f32[2,4,64]{2,1,0:T(4,128)}) custom-call(f32[256,128]{1,0:T(8,128)S(1)} %bitcast.14, f32[3,4,128,128]{3,2,1,0:T(8,128)S(1)} %get-tuple-element.17.product, f32[4,128]{1,0:T(4,128)S(1)} %get-tuple-element.18.free), custom_call_target="tpu_custom_call" | custom-call | tf_op jit(solution)/shard_map/finish/pallas_call | solution.py:383
  (4 shorter events, 0.0 us)
Async XLA Ops:
  1.3 1.7 %copy-start = (bf16[4,2,3,3,128,128]{5,4,3,2,1,0:T(8,128)(2,1)S(1)}, bf16[4,2,3,3,128,128]{5,4,3,2,1,0:T(8,128)(2,1)}, u32[]{:S(2)}) copy-start(bf16[4,2,3,3,128,128]{5,4,3,2,1,0:T(8,128)(2,1)} %history.1) | copy-start | bytes 7077892
  2.9 0.9 %copy-start.1 = (bf16[4,2,64,128]{3,2,1,0:T(8,128)(2,1)S(1)}, bf16[4,2,64,128]{3,2,1,0:T(8,128)(2,1)}, u32[]{:S(2)}) copy-start(bf16[4,2,64,128]{3,2,1,0:T(8,128)(2,1)} %pseudo.1) | copy-start | bytes 393220
  3.9 0.7 %copy-start.2 = (f32[4,3,128]{2,0,1:T(4,128)S(1)}, f32[4,3,128]{2,0,1:T(4,128)}, u32[]{:S(2)}) copy-start(f32[4,3,128]{2,0,1:T(4,128)} %param.11) | copy-start | bytes 18436
  4.5 0.7 %copy-start.3 = (bf16[4,2,3,3,128]{4,1,3,2,0:T(2,128)(2,1)S(1)}, bf16[4,2,3,3,128]{4,1,3,2,0:T(2,128)(2,1)}, u32[]{:S(2)}) copy-start(bf16[4,2,3,3,128]{4,1,3,2,0:T(2,128)(2,1)} %param.12) | copy-start | bytes 55300
  5.3 0.7 %copy-start.5 = (f32[2,64,4]{1,2,0:T(4,128)S(1)}, f32[2,64,4]{1,2,0:T(4,128)}, u32[]{:S(2)}) copy-start(f32[2,64,4]{1,2,0:T(4,128)} %param.18) | copy-start | bytes 6148
  6.0 32.0 %copy-start.4 = (f32[2,3,3,128]{3,0,2,1:T(2,128)S(1)}, f32[2,3,3,128]{3,0,2,1:T(2,128)}, u32[]{:S(2)}) copy-start(f32[2,3,3,128]{3,0,2,1:T(2,128)} %param.14) | copy-start | bytes 27652
  6.0 32.0 %copy-start.7 = (s32[128]{0:T(128)S(1)}, s32[128]{0:T(128)}, u32[]{:S(2)}) copy-start(s32[128]{0:T(128)} %param.15) | copy-start | bytes 1540
  6.0 43.6 %copy-start.6 = (s32[64,6]{0,1:T(8,128)S(1)}, s32[64,6]{0,1:T(8,128)}, u32[]{:S(2)}) copy-start(s32[64,6]{0,1:T(8,128)} %param.17) | copy-start | bytes 4612
  6.0 43.6 %copy-start.8 = (f32[64]{0:T(128)S(1)}, f32[64]{0:T(128)}, u32[]{:S(2)}) copy-start(f32[64]{0:T(128)} %param.16) | copy-start | bytes 772
  9.0 4.7 %collective-permute-start = (bf16[16,104,128]{2,1,0:T(8,128)(2,1)S(1)}, bf16[16,104,128]{2,1,0:T(8,128)(2,1)S(1)}, u32[]{:S(2)}, u32[]{:S(2)}) collective-permute-start(bf16[16,104,128]{2,1,0:T(8,128)(2,1)S(1)} %get-tuple-element.13), channel_id=1, source_target_pairs={{0,1},{1,0},{2,3},{3,2},{4,5},{5,4},{6,7},{7,6},{8,9},{9,8},{10,11... | collective-permute-start | bytes 1277960 | tf_op jit(solution)/shard_map/ppermute | solution.py:331
  38.9 23.4 %all-to-all-start.1 = ((f32[256,1,128]{2,1,0:T(1,128)}), f32[256,1,128]{2,1,0:T(1,128)S(1)}, u32[]{:S(2)}, u32[]{:S(2)}) async-start(f32[256,1,128]{2,1,0:T(1,128)} %bitcast.9), calls=%async_computation.1 | async-start | bytes 262144 | tf_op jit(solution)/shard_map/all_to_all | solution.py:361

commit v2 on v1

v2 whole, which is shorter than its diff:
```python
import jax
import jax.numpy as jnp
from jax import lax
from jax.experimental import pallas as pl
from jax.experimental.pallas import tpu as pltpu
from jax.sharding import PartitionSpec as P

time_step = 0.05
coupling = 0.02
F32 = jnp.float32
BF16 = jnp.bfloat16
HIGHEST = lax.Precision.HIGHEST
TERMS = 80
CHUNKS = 4


def flag(condition):
    return jnp.where(condition, 1.0, 0.0).astype(F32)


def low_half(lanes=128):
    return lax.broadcasted_iota(jnp.int32, (8, lanes), 0) < 4


def high_low(x):
    high = x.astype(BF16).astype(F32)
    return jnp.where(low_half(x.shape[1]), high, x - high)


def interleave(p, q):
    low = low_half(p.shape[1])
    return jnp.where(low, p, pltpu.roll(q, 4, 0)), jnp.where(low, pltpu.roll(p, 4, 0), q)


def terms_kernel(
    step, kernel_row, energy, history, own, other, current_row, kernel_here, energy_here, coeff, store, few, sems
):
    position = lax.axis_index("hist")
    wide = history.shape[4] // CHUNKS

    def fetch(i):
        columns = pl.ds(pl.multiple_of(i * wide, wide), wide)
        return pltpu.make_async_copy(
            history.at[:, :, :, :, columns, :], store.at[:, :, :, :, columns, :], sems.at[i]
        )

    small = [
        pltpu.make_async_copy(kernel_row, kernel_here, few.at[0]),
        pltpu.make_async_copy(energy, energy_here, few.at[1]),
    ]
    for copy in small:
        copy.start()
    for i in range(CHUNKS):
        fetch(i).start()
    for copy in small:
        copy.wait()
    current = step[0]
    block = energy.shape[1]
    lanes = energy.shape[2]
    current_row[...] = jnp.full((1, lanes), current, jnp.int32)
    zero = jnp.zeros((1, lanes), F32)
    total = jnp.zeros((3, lanes), F32)
    for m in range(block):
        time = position * block + m
        weight = jnp.where(time < current, jnp.where(time == 0, 0.5, 1.0), 0.0).astype(F32)
        total = total + energy_here[:, m, :] * flag(time < current)
        for a in range(3):
            for b in range(3):
                rows = kernel_here[m, a, b].astype(F32) * weight
                for s in range(2):
                    coeff[m, s, a, b] = jnp.broadcast_to(rows[s : s + 1], (8, lanes))
    energies = high_low(jnp.concatenate([total, zero, total, zero], axis=0))
    even_core = position % 2 == 0

    def sixteen(start, pair):
        groups = [[], []]
        for c in range(3):
            acc = {}
            for m in range(block):
                for b in range(3):
                    columns = pl.ds(pl.multiple_of(start, 16), 16)
                    re = store[m, 0, b, c, columns, :].astype(F32)
                    im = store[m, 1, b, c, columns, :].astype(F32)
                    for a in range(3):
                        kr = coeff[m, 0, a, b]
                        ki = coeff[m, 1, a, b]
                        for g in range(2):
                            hr, hi = re[8 * g : 8 * g + 8], im[8 * g : 8 * g + 8]
                            x = kr * hr - ki * hi
                            y = kr * hi + ki * hr
                            acc[0, a, g] = x if m + b == 0 else acc[0, a, g] + x
                            acc[1, a, g] = y if m + b == 0 else acc[1, a, g] + y
            for g in range(2):
                groups[g] += [acc[s, a, g] for s in range(2) for a in range(3)]
        for g in range(2):
            chip = pair + g
            evens, odds = [], []

            def add(p, q):
                x, y = interleave(p, q)
                evens.append(x)
                odds.append(y)

            for u in range(9):
                add(groups[g][2 * u], groups[g][2 * u + 1])
            evens.append(energies * flag(position > 2 * chip))
            odds.append(energies * flag(position > 2 * chip + 1))
            even = jnp.concatenate(evens, axis=0).astype(BF16)
            odd = jnp.concatenate(odds, axis=0).astype(BF16)
            own[chip] = jnp.where(even_core, even, odd)
            other[chip] = jnp.where(even_core, odd, even)

    @pl.loop(0, CHUNKS)
    def _(i):
        fetch(i).wait()

        @pl.loop(0, wide // 16)
        def _(h):
            sixteen(i * wide + h * 16, i * (wide // 8) + 2 * h)


def add_kernel(own, arrived, out):
    @pl.loop(0, own.shape[0] // 4)
    def _(i):
        for u in range(4):
            t = 4 * i + u
            x = own[t].astype(F32) + arrived[t].astype(F32)
            energies = x[72:80]
            energies = high_low(energies + pltpu.roll(energies, 4, 0))
            out[t] = jnp.concatenate([x[:72], energies], axis=0).astype(BF16)


def signed_swap(x):
    lanes = x.shape[1]
    swapped = pltpu.roll(x, lanes // 2, 1)
    lower = lax.broadcasted_iota(jnp.int32, x.shape, 1) < lanes // 2
    return jnp.where(lower, -swapped, swapped)


def ahead_kernel(step, predicted, pseudo, links, levels, turned, reached, free):
    current, position = step[...], lax.axis_index("hist")
    block, states = predicted.shape[1], predicted.shape[2]
    for m in range(block):
        both = jnp.concatenate([pseudo[m, 0], pseudo[m, 1]], axis=0).astype(F32)
        turned[m] = both.T
    column = lax.broadcasted_iota(jnp.int32, (block, 2 * states), 0) + position * block
    weight = jnp.where(column < current, jnp.where(column == 0, 0.5, 1.0), 0.0) * coupling
    state = lax.broadcasted_iota(jnp.int32, (states, states), 0)
    for a in range(3):
        link = flag(links[2 * a : 2 * a + 1, :] == state) + flag(links[2 * a + 1 : 2 * a + 2, :] == state)
        link = jnp.concatenate([link, link], axis=1)
        for p in range(2):
            x = jnp.concatenate([predicted[p], predicted[p]], axis=0)
            x = jnp.dot(x, link, precision=HIGHEST, preferred_element_type=F32)
            reached[a, p] = x[:block] * weight.astype(F32)
    elapsed = (current - column).astype(F32)
    level = jnp.concatenate([levels[...], levels[...]], axis=1)
    spin = level * time_step * elapsed
    lower = lax.broadcasted_iota(jnp.int32, spin.shape, 1) < states
    free[...] = jnp.where(lower, -jnp.sin(spin), -jnp.cos(spin)) * (column <= current).astype(F32)


def rows_kernel(step, arrived, energy, inverse, multiplicity, turned, reached, fresh, own, other):
    current, position = step[...], lax.axis_index("hist")
    block = energy.shape[1]
    lanes = energy.shape[2]
    got = arrived[0].astype(F32)
    for i in range(1, arrived.shape[0]):
        got = got + arrived[i].astype(F32)
    later = got[72:75] + got[76:79]
    ends = []
    for m in reversed(range(block)):
        later = later + energy[:, m, :] * flag(position * block + m < current)
        ends.append(later)
    angle = jnp.concatenate(
        [ends[block - 1 - j][a : a + 1] for a in range(3) for j in range(block)], axis=0
    )
    angle = angle * time_step
    column = lax.broadcasted_iota(jnp.int32, angle.shape, 0) % block + position * block
    in_range = (column <= current).astype(F32)
    free = [-jnp.sin(angle) * in_range, -jnp.cos(angle) * in_range]

    def right(s, b, c):
        r = ((c * 2 + s) * 3 + b) * block
        x = got[r : r + block]
        return x + free[s][b * block : (b + 1) * block] if b == c else x

    entries = {}
    for c in range(3):
        side = {(s, b): right(s, b, c) for s in range(2) for b in range(3)}
        for a in range(3):
            re = im = 0.0
            for b in range(3):
                dr, di = inverse[a, b, 0:1, :], inverse[a, b, 1:2, :]
                re = re + dr * side[0, b] - di * side[1, b]
                im = im + dr * side[1, b] + di * side[0, b]
            entries[a, c, 0], entries[a, c, 1] = re, im
    entries = [entries[a, c, s] for a in range(3) for c in range(3) for s in range(2)]
    for i, x in enumerate(entries):
        fresh[i] = x
    shared = multiplicity[...].astype(F32)
    even_core = position % 2 == 0
    real = imag = 0.0
    for a in range(3):
        re = jnp.sum(entries[8 * a] * shared, axis=1, keepdims=True)
        im = jnp.sum(entries[8 * a + 1] * shared, axis=1, keepdims=True)
        real = real + re * reached[a, 0] - im * reached[a, 1]
        imag = imag + re * reached[a, 1] + im * reached[a, 0]
    entries += [jnp.ones((1, lanes), F32), jnp.zeros((lanes - 73, lanes), F32)]
    table = jnp.concatenate(entries, axis=0)
    weights = jnp.broadcast_to(shared, (8, lanes))
    message = lax.dot_general(
        weights, table, (((1,), (1,)), ((), ())), precision=HIGHEST, preferred_element_type=F32
    )[0:1]
    high = message.astype(BF16).astype(F32)
    message = jnp.concatenate([high, message - high], axis=0)
    for t in range(own.shape[0]):
        x = y = 0.0
        for m in range(block):
            past = turned[m, 8 * t : 8 * t + 8, :]
            x = x + real[m : m + 1] * past
            y = y + imag[m : m + 1] * past
        x = x + signed_swap(y)
        tile = []
        for core in range(2):
            pairs = [x[4 * core : 4 * core + 2], x[4 * core + 2 : 4 * core + 4]]
            pairs.append(message * flag(position == 2 * t + core))
            tile.append(jnp.concatenate(pairs, axis=1).astype(BF16))
        own[t] = jnp.where(even_core, tile[0], tile[1])
        other[t] = jnp.where(even_core, tile[1], tile[0])


def add_shares_kernel(own, arrived, out):
    for t in range(own.shape[0]):
        tile = (own[t].astype(F32) + arrived[t].astype(F32)).astype(BF16)
        for k in range(out.shape[0]):
            out[k, t] = tile


def lattice_kernel(fresh, lattice):
    for a in range(3):
        for c in range(3):
            i = (a * 3 + c) * 2
            re, im = fresh[i], fresh[i + 1]
            for j in range(lattice.shape[0]):
                pair = jnp.concatenate([re[j : j + 1], im[j : j + 1]], axis=0)
                lattice[j, a, c] = pair.astype(BF16)


def finish_kernel(got, free, local, pseudo):
    parts = []
    for i in range(4):
        x = got[i].astype(F32)
        for k in range(i + 4, got.shape[0], 4):
            x = x + got[k].astype(F32)
        parts.append(x)
    total = (parts[0] + parts[1]) + (parts[2] + parts[3])
    lanes = free.shape[1]
    states = lanes // 2
    sums = total[0:1, 2 * lanes :] + total[1:2, 2 * lanes :]
    count = sums[:, 72:73]
    mean = sums / count
    for a in range(3):
        for c in range(3):
            i = (a * 3 + c) * 8
            local[a, c] = jnp.concatenate([mean[:, i : i + 4], mean[:, i + 4 : i + 8]], axis=0)
    shares = jnp.concatenate([total[:, :lanes], total[:, lanes : 2 * lanes]], axis=0)
    out = free[...] + shares / count
    pseudo[0] = out[:, :states]
    pseudo[1] = out[:, states:]


VMEM = pl.BlockSpec(memory_space=pltpu.VMEM)
HBM = pl.BlockSpec(memory_space=pltpu.HBM)


def grant(mib):
    return pltpu.CompilerParams(vmem_limit_bytes=mib << 20)


def in_hbm(x):
    return pltpu.with_memory_space_constraint(x, pltpu.HBM)


def per_device(
    step_index,
    band_energy,
    kernel_row,
    lattice_history,
    diagonal_inverse,
    multiplicity,
    state_energy,
    connection,
    predicted_row,
    pseudo_history,
):
    block, _, lanes = band_energy.shape
    states, flavours = connection.shape
    ka_size, hist_size = lax.axis_size("ka"), lax.axis_size("hist")
    chips = hist_size // 2
    energy = jnp.transpose(band_energy, (1, 0, 2))
    kernel_pairs = jnp.transpose(kernel_row, (0, 2, 3, 1, 4))
    tiles = jax.ShapeDtypeStruct((chips, TERMS, lanes), BF16)
    cores = [(h, h ^ 1) for h in range(hist_size)]

    own, other, step = pl.pallas_call(
        terms_kernel,
        out_shape=(tiles, tiles, jax.ShapeDtypeStruct((1, lanes), jnp.int32)),
        in_specs=[pl.BlockSpec(memory_space=pltpu.SMEM), HBM, HBM, HBM],
        out_specs=(VMEM, VMEM, VMEM),
        scratch_shapes=[
            pltpu.VMEM(kernel_pairs.shape, BF16),
            pltpu.VMEM(energy.shape, F32),
            pltpu.VMEM((block, 2, 3, 3, 8, lanes), F32),
            pltpu.VMEM(lattice_history.shape, BF16),
            pltpu.SemaphoreType.DMA((2,)),
            pltpu.SemaphoreType.DMA((CHUNKS,)),
        ],
        compiler_params=grant(16),
        name="terms",
    )(step_index, in_hbm(kernel_pairs), in_hbm(energy), in_hbm(lattice_history))
    swapped = lax.ppermute(other, "hist", cores)
    paired = pl.pallas_call(
        add_kernel,
        out_shape=tiles,
        in_specs=[VMEM, VMEM],
        out_specs=VMEM,
        compiler_params=grant(8),
        name="add_pair",
    )(own, swapped)
    same_core = [[2 * t + c for t in range(chips)] for c in range(2)]
    arrived = lax.all_to_all(
        paired, "hist", split_axis=0, concat_axis=0, tiled=True, axis_index_groups=same_core
    )
    turned, reached, free = pl.pallas_call(
        ahead_kernel,
        out_shape=(
            jax.ShapeDtypeStruct((block, block * hist_size, 2 * states), F32),
            jax.ShapeDtypeStruct((3, 2, block, 2 * states), F32),
            jax.ShapeDtypeStruct((block, 2 * states), F32),
        ),
        in_specs=[VMEM, VMEM, VMEM, VMEM, VMEM],
        out_specs=(VMEM, VMEM, VMEM),
        compiler_params=grant(8),
        cost_estimate=pl.CostEstimate(flops=4_000_000, bytes_accessed=400_000, transcendentals=1024),
        name="ahead",
    )(
        step,
        jnp.transpose(predicted_row, (0, 2, 1)),
        pseudo_history,
        connection.T,
        state_energy.reshape(1, states),
    )
    shares = jax.ShapeDtypeStruct((chips, 2, 3 * lanes), BF16)
    fresh, own, other = pl.pallas_call(
        rows_kernel,
        out_shape=(jax.ShapeDtypeStruct((18, block, lanes), F32), shares, shares),
        in_specs=[VMEM, VMEM, VMEM, VMEM, VMEM, VMEM, VMEM],
        out_specs=(VMEM, VMEM, VMEM),
        compiler_params=grant(8),
        name="rows",
    )(
        step,
        arrived,
        energy,
        jnp.transpose(diagonal_inverse, (1, 2, 0, 3)),
        multiplicity.reshape(1, lanes),
        turned,
        reached,
    )
    swapped = lax.ppermute(other, "hist", cores)
    paired = pl.pallas_call(
        add_shares_kernel,
        out_shape=jax.ShapeDtypeStruct((ka_size, *shares.shape), BF16),
        in_specs=[VMEM, VMEM],
        out_specs=VMEM,
        compiler_params=grant(8),
        name="add_shares",
    )(own, swapped)
    same_core = [
        [k * hist_size + 2 * t + c for k in range(ka_size) for t in range(chips)] for c in range(2)
    ]
    got = lax.all_to_all(
        paired.reshape(ka_size * chips, 2, 3 * lanes),
        ("ka", "hist"),
        split_axis=0,
        concat_axis=0,
        tiled=True,
        axis_index_groups=same_core,
    )
    lattice = pl.pallas_call(
        lattice_kernel,
        out_shape=jax.ShapeDtypeStruct((block, 3, 3, 2, lanes), BF16),
        in_specs=[VMEM],
        out_specs=VMEM,
        compiler_params=grant(8),
        cost_estimate=pl.CostEstimate(flops=10_000, bytes_accessed=60_000, transcendentals=0),
        name="lattice",
    )(fresh)
    local, pseudo = pl.pallas_call(
        finish_kernel,
        out_shape=(
            jax.ShapeDtypeStruct((3, 3, 2, block), F32),
            jax.ShapeDtypeStruct((2, block, states), F32),
        ),
        in_specs=[VMEM, VMEM],
        out_specs=(VMEM, VMEM),
        compiler_params=grant(8),
        name="finish",
    )(got, free)
    return (
        jnp.transpose(lattice, (0, 3, 1, 2, 4)),
        jnp.transpose(local, (2, 0, 1, 3)),
        jnp.transpose(pseudo, (0, 2, 1)),
    )


def solution(mesh):
    in_specs = (
        P(),
        P("hist", None, "ka"),
        P("hist", None, None, None, "ka"),
        P("hist", None, None, None, None, "ka"),
        P(None, None, None, "ka"),
        P("ka"),
        P(),
        P(),
        P(None, None, "hist"),
        P("hist", None, None, None),
    )
    out_specs = (
        P("hist", None, None, None, "ka"),
        P(None, None, None, "hist"),
        P(None, None, "hist"),
    )
    return jax.shard_map(
        per_device, mesh=mesh, in_specs=in_specs, out_specs=out_specs, check_vma=False
    )
```

time: 63.6 us -> 58.2 us (0.915)
  blocking collectives: 24.1 us -> 0 us
  waiting for transfers between devices: 11.7 us -> 25 us
  starting transfers between devices: 13.9 us -> 24 us
  local copies, waits for them, and re-layouts: 4.68 us -> 0.03 us
    all_to_all x1 -> x0, blocking collectives: 24.1 us -> none  [per_device(): lax.all_to_all(paired, 'hist', split_axis=0, concat_axis=0, tiled=True, a...]
    all_to_all x1 -> x2, waiting for transfers between devices: 10.3 us -> 22.8 us  [the longest x1 11.8 us: per_device(): lax.all_to_all(paired.reshape(ka_size * chips, 2, 3 * lanes), ('ka', 'his...]
    all_to_all x1 -> x2, starting transfers between devices: 10.6 us -> 18.2 us  [the longest x1 9.18 us: per_device(): lax.all_to_all(paired, 'hist', split_axis=0, concat_axis=0, tiled=True, a...]
    unnamed x18 -> x14, local copies, waits for them, and re-layouts: 4.68 us -> 0.03 us
    ppermute x1 -> x2, starting transfers between devices: 3.33 us -> 5.83 us  [per_device(): swapped = lax.ppermute(other, 'hist', cores)]
    ppermute x1 -> x2, waiting for transfers between devices: 1.4 us -> 2.11 us  [per_device(): swapped = lax.ppermute(other, 'hist', cores)]
    pallas_call x3 -> x5, Pallas kernels: 5.68 us -> 6.22 us  [the longest x1 3.66 us: per_device(): pl.pallas_call(terms_kernel, out_shape=(tiles, tiles, jax.ShapeDtypeStruc...]
  transfers between devices with their start and end apart: 2 -> 4, of which waited for: 2 -> 4; matrix products, arithmetic and copies ran while one was open for 0% -> 0% of each run, Pallas kernels for 4% -> 2%
where the time goes in v2:
time: 58.2 us; the launch traced here: 57.9 us
  waiting for transfers between devices  25 us (43%)
  starting transfers between devices  24 us (41%)
  Pallas kernels  7.46 us (13%)
  between operations  1.47 us (3%)
    all_to_all x1, waiting for transfers between devices, per_device(): lax.all_to_all(paired.reshape(ka_size * chips, 2, 3 * lanes), ('ka', 'his...  11.8 us
    all_to_all x1, waiting for transfers between devices, per_device(): lax.all_to_all(paired, 'hist', split_axis=0, concat_axis=0, tiled=True, a...  11 us
    all_to_all x1, starting transfers between devices, per_device(): lax.all_to_all(paired, 'hist', split_axis=0, concat_axis=0, tiled=True, a...  9.18 us
    all_to_all x1, starting transfers between devices, per_device(): lax.all_to_all(paired.reshape(ka_size * chips, 2, 3 * lanes), ('ka', 'his...  8.98 us
    ppermute x2, starting transfers between devices, per_device(): swapped = lax.ppermute(other, 'hist', cores)  5.83 us
    pallas_call x1, Pallas kernels, per_device(): pl.pallas_call(terms_kernel, out_shape=(tiles, tiles, jax.ShapeDtypeStruc...  3.66 us
    ppermute x2, waiting for transfers between devices, per_device(): swapped = lax.ppermute(other, 'hist', cores)  2.11 us
  transfers between devices with their start and end apart: 4, of which 4 were waited for; matrix products, arithmetic and copies ran while one was open for 0% of the time, Pallas kernels for 2%

profile of v2, /device:TPU:1, one launch (start us, length us, event | category | flops | bytes accessed | tf_op | source)
XLA Modules:
  0.0 57.9 jit_solution(14990071511406352448)
XLA Ops:
  0.6 0.0 copy-start.1
  0.6 0.0 copy-start.3
  0.7 0.0 copy-start
  0.7 0.0 copy-start.4
  0.7 0.0 copy-start.5
  0.7 0.0 copy-start.2
  0.7 0.0 copy-start.6
  1.4 3.7 %terms.1 = (bf16[16,80,128]{2,1,0:T(8,128)(2,1)S(1)}, bf16[16,80,128]{2,1,0:T(8,128)(2,1)S(1)}, s32[1,128]{1,0:T(1,128)S(1)}) custom-call(s32[1]{0:T(128)S(6)} %copy.13.step, bf16[4,3,3,2,128]{4,3,2,1,0:T(2,128)(2,1)} %bitcast.19, f32[3,4,128]{2,1,0:T(4,128)} %bitcast.11, bf16[4,2,3,3,128,128]{5,4,3,2,1,0:T(8,128)(2,1)} %history.1), custom_call_target="tpu_custom_call" | custom-call | tf_op jit(solution)/shard_map/terms/pallas_call | solution.py:306
  5.1 3.3 %collective-permute-start = (bf16[16,80,128]{2,1,0:T(8,128)(2,1)S(1)}, bf16[16,80,128]{2,1,0:T(8,128)(2,1)S(1)}, u32[]{:S(2)}, u32[]{:S(2)}) collective-permute-start(bf16[16,80,128]{2,1,0:T(8,128)(2,1)S(1)} %get-tuple-element.16), channel_id=1, source_target_pairs={{0,1},{1,0},{2,3},{3,2},{4,5},{5,4},{6,7},{7,6},{8,9},{9,8},{10,11... | collective-permute-start | bytes 983048 | tf_op jit(solution)/shard_map/ppermute | solution.py:322
  8.4 1.3 %collective-permute-done.arrived = bf16[16,80,128]{2,1,0:T(8,128)(2,1)S(1)} collective-permute-done((bf16[16,80,128]{2,1,0:T(8,128)(2,1)S(1)}, bf16[16,80,128]{2,1,0:T(8,128)(2,1)S(1)}, u32[]{:S(2)}, u32[]{:S(2)}) %collective-permute-start) | collective-permute-done | bytes 327712 | tf_op jit(solution)/shard_map/ppermute | solution.py:322
  9.7 0.8 %add_pair.1 = bf16[16,80,128]{2,1,0:T(8,128)(2,1)} custom-call(bf16[16,80,128]{2,1,0:T(8,128)(2,1)S(1)} %get-tuple-element.15.own, bf16[16,80,128]{2,1,0:T(8,128)(2,1)S(1)} %collective-permute-done.arrived), custom_call_target="tpu_custom_call" | custom-call | tf_op jit(solution)/shard_map/add_pair/pallas_call | solution.py:323
  10.5 9.2 %all-to-all-start = ((bf16[16,80,128]{2,1,0:T(8,128)(2,1)}), bf16[16,80,128]{2,1,0:T(8,128)(2,1)S(1)}, u32[]{:S(2)}, u32[]{:S(2)}) async-start(bf16[16,80,128]{2,1,0:T(8,128)(2,1)} %add_pair.1), calls=%async_computation | async-start | bytes 655360 | tf_op jit(solution)/shard_map/all_to_all | solution.py:332
  19.7 0.0 copy-done.3
  19.7 0.0 copy-done
  19.7 0.3 ahead.1
  20.1 11.0 %all-to-all-done.arrived = bf16[16,80,128]{2,1,0:T(8,128)(2,1)S(1)} async-done(((bf16[16,80,128]{2,1,0:T(8,128)(2,1)}), bf16[16,80,128]{2,1,0:T(8,128)(2,1)S(1)}, u32[]{:S(2)}, u32[]{:S(2)}) %all-to-all-start) | async-done | bytes 327712 | tf_op jit(solution)/shard_map/all_to_all | solution.py:332
  31.1 0.4 rows.1
  31.5 2.5 %collective-permute-start.1 = (bf16[16,2,384]{2,1,0:T(2,128)(2,1)S(1)}, bf16[16,2,384]{2,1,0:T(2,128)(2,1)S(1)}, u32[]{:S(2)}, u32[]{:S(2)}) collective-permute-start(bf16[16,2,384]{2,1,0:T(2,128)(2,1)S(1)} %get-tuple-element.21), channel_id=1, source_target_pairs={{0,1},{1,0},{2,3},{3,2},{4,5},{5,4},{6,7},{7,6},{8,9},{9,8},{10,11... | collective-permute-start | bytes 73736 | tf_op jit(solution)/shard_map/ppermute | solution.py:371
  34.0 0.8 %collective-permute-done.1.arrived = bf16[16,2,384]{2,1,0:T(2,128)(2,1)S(1)} collective-permute-done((bf16[16,2,384]{2,1,0:T(2,128)(2,1)S(1)}, bf16[16,2,384]{2,1,0:T(2,128)(2,1)S(1)}, u32[]{:S(2)}, u32[]{:S(2)}) %collective-permute-start.1) | collective-permute-done | bytes 24608 | tf_op jit(solution)/shard_map/ppermute | solution.py:371
  34.8 0.8 %add_shares.1 = bf16[8,16,2,384]{3,2,1,0:T(2,128)(2,1)} custom-call(bf16[16,2,384]{2,1,0:T(2,128)(2,1)S(1)} %get-tuple-element.20.own, bf16[16,2,384]{2,1,0:T(2,128)(2,1)S(1)} %collective-permute-done.1.arrived), custom_call_target="tpu_custom_call" | custom-call | tf_op jit(solution)/shard_map/add_shares/pallas_call | solution.py:372
  35.6 9.0 %all-to-all-start.1 = ((bf16[128,2,384]{2,1,0:T(2,128)(2,1)}), bf16[128,2,384]{2,1,0:T(2,128)(2,1)S(1)}, u32[]{:S(2)}, u32[]{:S(2)}) async-start(bf16[128,2,384]{2,1,0:T(2,128)(2,1)} %bitcast.8), calls=%async_computation.1 | async-start | bytes 393216 | tf_op jit(solution)/shard_map/all_to_all | solution.py:383
  44.6 0.6 %lattice.1 = bf16[4,3,3,2,128]{4,3,2,1,0:T(2,128)(2,1)} custom-call(f32[18,4,128]{2,1,0:T(4,128)S(1)} %get-tuple-element.19.fresh), custom_call_target="tpu_custom_call" | custom-call | flops 10000 | bytes 60000 | tf_op jit(solution)/shard_map/lattice/pallas_call | solution.py:391
  45.2 11.8 %all-to-all-done.1.got = bf16[128,2,384]{2,1,0:T(2,128)(2,1)S(1)} async-done(((bf16[128,2,384]{2,1,0:T(2,128)(2,1)}), bf16[128,2,384]{2,1,0:T(2,128)(2,1)S(1)}, u32[]{:S(2)}, u32[]{:S(2)}) %all-to-all-start.1) | async-done | bytes 196640 | tf_op jit(solution)/shard_map/all_to_all | solution.py:383
  57.0 0.9 %finish.1 = (f32[3,3,2,4]{3,2,1,0:T(2,128)}, f32[2,4,64]{2,1,0:T(4,128)}) custom-call(bf16[128,2,384]{2,1,0:T(2,128)(2,1)S(1)} %all-to-all-done.1.got, f32[4,128]{1,0:T(4,128)S(1)} %get-tuple-element.22.free), custom_call_target="tpu_custom_call" | custom-call | tf_op jit(solution)/shard_map/finish/pallas_call | solution.py:400
  (5 shorter events, 0.0 us)
Async XLA Ops:
  0.6 30.5 %copy-start.1 = (f32[4,3,128]{2,0,1:T(4,128)S(1)}, f32[4,3,128]{2,0,1:T(4,128)}, u32[]{:S(2)}) copy-start(f32[4,3,128]{2,0,1:T(4,128)} %param.11) | copy-start | bytes 18436
  0.6 19.1 %copy-start.3 = (f32[2,64,4]{1,2,0:T(4,128)S(1)}, f32[2,64,4]{1,2,0:T(4,128)}, u32[]{:S(2)}) copy-start(f32[2,64,4]{1,2,0:T(4,128)} %param.18) | copy-start | bytes 6148
  0.7 19.1 %copy-start = (bf16[4,2,64,128]{3,2,1,0:T(8,128)(2,1)S(1)}, bf16[4,2,64,128]{3,2,1,0:T(8,128)(2,1)}, u32[]{:S(2)}) copy-start(bf16[4,2,64,128]{3,2,1,0:T(8,128)(2,1)} %pseudo.1) | copy-start | bytes 393220
  0.7 19.1 %copy-start.4 = (s32[64,6]{0,1:T(8,128)S(1)}, s32[64,6]{0,1:T(8,128)}, u32[]{:S(2)}) copy-start(s32[64,6]{0,1:T(8,128)} %param.17) | copy-start | bytes 4612
  0.7 19.1 %copy-start.5 = (f32[64]{0:T(128)S(1)}, f32[64]{0:T(128)}, u32[]{:S(2)}) copy-start(f32[64]{0:T(128)} %param.16) | copy-start | bytes 772
  0.7 30.4 %copy-start.2 = (f32[2,3,3,128]{3,0,2,1:T(2,128)S(1)}, f32[2,3,3,128]{3,0,2,1:T(2,128)}, u32[]{:S(2)}) copy-start(f32[2,3,3,128]{3,0,2,1:T(2,128)} %param.14) | copy-start | bytes 27652
  0.7 30.4 %copy-start.6 = (s32[128]{0:T(128)S(1)}, s32[128]{0:T(128)}, u32[]{:S(2)}) copy-start(s32[128]{0:T(128)} %param.15) | copy-start | bytes 1540
  5.1 4.6 %collective-permute-start = (bf16[16,80,128]{2,1,0:T(8,128)(2,1)S(1)}, bf16[16,80,128]{2,1,0:T(8,128)(2,1)S(1)}, u32[]{:S(2)}, u32[]{:S(2)}) collective-permute-start(bf16[16,80,128]{2,1,0:T(8,128)(2,1)S(1)} %get-tuple-element.16), channel_id=1, source_target_pairs={{0,1},{1,0},{2,3},{3,2},{4,5},{5,4},{6,7},{7,6},{8,9},{9,8},{10,11... | collective-permute-start | bytes 983048 | tf_op jit(solution)/shard_map/ppermute | solution.py:322
  10.5 20.6 %all-to-all-start = ((bf16[16,80,128]{2,1,0:T(8,128)(2,1)}), bf16[16,80,128]{2,1,0:T(8,128)(2,1)S(1)}, u32[]{:S(2)}, u32[]{:S(2)}) async-start(bf16[16,80,128]{2,1,0:T(8,128)(2,1)} %add_pair.1), calls=%async_computation | async-start | bytes 655360 | tf_op jit(solution)/shard_map/all_to_all | solution.py:332
  31.5 3.4 %collective-permute-start.1 = (bf16[16,2,384]{2,1,0:T(2,128)(2,1)S(1)}, bf16[16,2,384]{2,1,0:T(2,128)(2,1)S(1)}, u32[]{:S(2)}, u32[]{:S(2)}) collective-permute-start(bf16[16,2,384]{2,1,0:T(2,128)(2,1)S(1)} %get-tuple-element.21), channel_id=1, source_target_pairs={{0,1},{1,0},{2,3},{3,2},{4,5},{5,4},{6,7},{7,6},{8,9},{9,8},{10,11... | collective-permute-start | bytes 73736 | tf_op jit(solution)/shard_map/ppermute | solution.py:371
  35.6 21.4 %all-to-all-start.1 = ((bf16[128,2,384]{2,1,0:T(2,128)(2,1)}), bf16[128,2,384]{2,1,0:T(2,128)(2,1)S(1)}, u32[]{:S(2)}, u32[]{:S(2)}) async-start(bf16[128,2,384]{2,1,0:T(2,128)(2,1)} %bitcast.8), calls=%async_computation.1 | async-start | bytes 393216 | tf_op jit(solution)/shard_map/all_to_all | solution.py:383

commit v3 on v2

--- a/solution.py
+++ b/solution.py
@@ -67,8 +67,9 @@
         for a in range(3):
             for b in range(3):
                 rows = kernel_here[m, a, b].astype(F32) * weight
-                for s in range(2):
-                    coeff[m, s, a, b] = jnp.broadcast_to(rows[s : s + 1], (8, lanes))
+                re, im = rows[0:1], rows[1:2]
+                for i, x in enumerate((re, re + im, im - re)):
+                    coeff[m, i, a, b] = jnp.broadcast_to(x, (8, lanes))
     energies = high_low(jnp.concatenate([total, zero, total, zero], axis=0))
     even_core = position % 2 == 0
 
@@ -81,15 +82,18 @@
                     columns = pl.ds(pl.multiple_of(start, 16), 16)
                     re = store[m, 0, b, c, columns, :].astype(F32)
                     im = store[m, 1, b, c, columns, :].astype(F32)
+                    both = re + im
                     for a in range(3):
-                        kr = coeff[m, 0, a, b]
-                        ki = coeff[m, 1, a, b]
+                        weights = [coeff[m, i, a, b] for i in range(3)]
                         for g in range(2):
-                            hr, hi = re[8 * g : 8 * g + 8], im[8 * g : 8 * g + 8]
-                            x = kr * hr - ki * hi
-                            y = kr * hi + ki * hr
-                            acc[0, a, g] = x if m + b == 0 else acc[0, a, g] + x
-                            acc[1, a, g] = y if m + b == 0 else acc[1, a, g] + y
+                            rows = slice(8 * g, 8 * g + 8)
+                            for i, x in enumerate((both, im, re)):
+                                x = weights[i] * x[rows]
+                                acc[i, a, g] = x if m + b == 0 else acc[i, a, g] + x
+            for a in range(3):
+                for g in range(2):
+                    x = acc[0, a, g]
+                    acc[0, a, g], acc[1, a, g] = x - acc[1, a, g], x + acc[2, a, g]
             for g in range(2):
                 groups[g] += [acc[s, a, g] for s in range(2) for a in range(3)]
         for g in range(2):
@@ -119,7 +123,7 @@
             sixteen(i * wide + h * 16, i * (wide // 8) + 2 * h)
 
 
-def add_kernel(own, arrived, out):
+def add_kernel(own, arrived, _, out):
     @pl.loop(0, own.shape[0] // 4)
     def _(i):
         for u in range(4):
@@ -230,14 +234,15 @@
         other[t] = jnp.where(even_core, tile[1], tile[0])
 
 
-def add_shares_kernel(own, arrived, out):
+def add_shares_kernel(own, arrived, _, out):
     for t in range(own.shape[0]):
         tile = (own[t].astype(F32) + arrived[t].astype(F32)).astype(BF16)
         for k in range(out.shape[0]):
             out[k, t] = tile
 
 
-def lattice_kernel(fresh, lattice):
+def lattice_kernel(fresh, lattice, written):
+    written[...] = fresh[0, 0:1]
     for a in range(3):
         for c in range(3):
             i = (a * 3 + c) * 2
@@ -272,6 +277,7 @@
 
 VMEM = pl.BlockSpec(memory_space=pltpu.VMEM)
 HBM = pl.BlockSpec(memory_space=pltpu.HBM)
+ANY = pl.BlockSpec(memory_space=pl.ANY)
 
 
 def grant(mib):
@@ -311,7 +317,7 @@
         scratch_shapes=[
             pltpu.VMEM(kernel_pairs.shape, BF16),
             pltpu.VMEM(energy.shape, F32),
-            pltpu.VMEM((block, 2, 3, 3, 8, lanes), F32),
+            pltpu.VMEM((block, 3, 3, 3, 8, lanes), F32),
             pltpu.VMEM(lattice_history.shape, BF16),
             pltpu.SemaphoreType.DMA((2,)),
             pltpu.SemaphoreType.DMA((CHUNKS,)),
@@ -320,18 +326,6 @@
         name="terms",
     )(step_index, in_hbm(kernel_pairs), in_hbm(energy), in_hbm(lattice_history))
     swapped = lax.ppermute(other, "hist", cores)
-    paired = pl.pallas_call(
-        add_kernel,
-        out_shape=tiles,
-        in_specs=[VMEM, VMEM],
-        out_specs=VMEM,
-        compiler_params=grant(8),
-        name="add_pair",
-    )(own, swapped)
-    same_core = [[2 * t + c for t in range(chips)] for c in range(2)]
-    arrived = lax.all_to_all(
-        paired, "hist", split_axis=0, concat_axis=0, tiled=True, axis_index_groups=same_core
-    )
     turned, reached, free = pl.pallas_call(
         ahead_kernel,
         out_shape=(
@@ -351,6 +345,18 @@
         connection.T,
         state_energy.reshape(1, states),
     )
+    paired = pl.pallas_call(
+        add_kernel,
+        out_shape=tiles,
+        in_specs=[VMEM, VMEM, ANY],
+        out_specs=VMEM,
+        compiler_params=grant(8),
+        name="add_pair",
+    )(own, swapped, free)
+    same_core = [[2 * t + c for t in range(chips)] for c in range(2)]
+    arrived = lax.all_to_all(
+        paired, "hist", split_axis=0, concat_axis=0, tiled=True, axis_index_groups=same_core
+    )
     shares = jax.ShapeDtypeStruct((chips, 2, 3 * lanes), BF16)
     fresh, own, other = pl.pallas_call(
         rows_kernel,
@@ -369,14 +375,26 @@
         reached,
     )
     swapped = lax.ppermute(other, "hist", cores)
+    lattice, written = pl.pallas_call(
+        lattice_kernel,
+        out_shape=(
+            jax.ShapeDtypeStruct((block, 3, 3, 2, lanes), BF16),
+            jax.ShapeDtypeStruct((1, lanes), F32),
+        ),
+        in_specs=[VMEM],
+        out_specs=(VMEM, VMEM),
+        compiler_params=grant(8),
+        cost_estimate=pl.CostEstimate(flops=10_000, bytes_accessed=60_000, transcendentals=0),
+        name="lattice",
+    )(fresh)
     paired = pl.pallas_call(
         add_shares_kernel,
         out_shape=jax.ShapeDtypeStruct((ka_size, *shares.shape), BF16),
-        in_specs=[VMEM, VMEM],
+        in_specs=[VMEM, VMEM, ANY],
         out_specs=VMEM,
         compiler_params=grant(8),
         name="add_shares",
-    )(own, swapped)
+    )(own, swapped, written)
     same_core = [
         [k * hist_size + 2 * t + c for k in range(ka_size) for t in range(chips)] for c in range(2)
     ]
@@ -388,15 +406,6 @@
         tiled=True,
         axis_index_groups=same_core,
     )
-    lattice = pl.pallas_call(
-        lattice_kernel,
-        out_shape=jax.ShapeDtypeStruct((block, 3, 3, 2, lanes), BF16),
-        in_specs=[VMEM],
-        out_specs=VMEM,
-        compiler_params=grant(8),
-        cost_estimate=pl.CostEstimate(flops=10_000, bytes_accessed=60_000, transcendentals=0),
-        name="lattice",
-    )(fresh)
     local, pseudo = pl.pallas_call(
         finish_kernel,
         out_shape=(

time: 58.2 us -> 56 us (0.962)
  blocking collectives: 0 us -> 41.7 us
  waiting for transfers between devices: 25 us -> 1.13 us
  starting transfers between devices: 24 us -> 5.83 us
  Pallas kernels: 7.46 us -> 5.77 us
    all_to_all x0 -> x2, blocking collectives: none -> 41.7 us  [the longest x1 21.3 us: per_device(): lax.all_to_all(paired.reshape(ka_size * chips, 2, 3 * lanes), ('ka', 'his...]
    all_to_all x2 -> x0, waiting for transfers between devices: 22.8 us -> none  [the longest x1 11.8 us: per_device(): lax.all_to_all(paired.reshape(ka_size * chips, 2, 3 * lanes), ('ka', 'his...]
    all_to_all x2 -> x0, starting transfers between devices: 18.2 us -> none  [the longest x1 9.18 us: per_device(): lax.all_to_all(paired, 'hist', split_axis=0, concat_axis=0, tiled=True, a...]
    ppermute x2, waiting for transfers between devices: 2.11 us -> 1.13 us  [per_device(): swapped = lax.ppermute(other, 'hist', cores)]
    pallas_call x2, Pallas kernels: 1.47 us -> 0.75 us  [the longest x1 0.62 us: per_device(): pl.pallas_call(lattice_kernel, out_shape=(jax.ShapeDtypeStruct((block, 3,...]
    pallas_call x1, Pallas kernels: 0.75 us -> 0.08 us  [per_device(): pl.pallas_call(add_shares_kernel, out_shape=jax.ShapeDtypeStruct((ka_size...]
  transfers between devices with their start and end apart: 4 -> 2, of which waited for: 4 -> 2; matrix products, arithmetic and copies ran while one was open for 0% -> 0% of each run, Pallas kernels for 2% -> 2%
where the time goes in v3:
time: 56 us; the launch traced here: 55.8 us
  blocking collectives  41.7 us (74%)
  starting transfers between devices  5.83 us (10%)
  Pallas kernels  5.77 us (10%)
  between operations  1.43 us (3%)
  waiting for transfers between devices  1.13 us (2%)
    all_to_all x1, blocking collectives, per_device(): lax.all_to_all(paired.reshape(ka_size * chips, 2, 3 * lanes), ('ka', 'his...  21.3 us
    all_to_all x1, blocking collectives, per_device(): lax.all_to_all(paired, 'hist', split_axis=0, concat_axis=0, tiled=True, a...  20.4 us
    ppermute x2, starting transfers between devices, per_device(): swapped = lax.ppermute(other, 'hist', cores)  5.83 us
    pallas_call x1, Pallas kernels, per_device(): pl.pallas_call(terms_kernel, out_shape=(tiles, tiles, jax.ShapeDtypeStruc...  3.36 us
    ppermute x2, waiting for transfers between devices, per_device(): swapped = lax.ppermute(other, 'hist', cores)  1.13 us
  transfers between devices with their start and end apart: 2, of which 2 were waited for; matrix products, arithmetic and copies ran while one was open for 0% of the time, Pallas kernels for 2%

profile of v3, /device:TPU:1, one launch (start us, length us, event | category | flops | bytes accessed | tf_op | source)
XLA Modules:
  0.0 55.8 jit_solution(7355322642841316636)
XLA Ops:
  0.6 0.0 copy-start.1
  0.6 0.0 copy-start.3
  0.7 0.0 copy-start
  0.7 0.0 copy-start.4
  0.7 0.0 copy-start.5
  0.7 0.0 copy-start.2
  0.7 0.0 copy-start.6
  1.4 3.4 %terms.1 = (bf16[16,80,128]{2,1,0:T(8,128)(2,1)S(1)}, bf16[16,80,128]{2,1,0:T(8,128)(2,1)S(1)}, s32[1,128]{1,0:T(1,128)S(1)}) custom-call(s32[1]{0:T(128)S(6)} %copy.13.step, bf16[4,3,3,2,128]{4,3,2,1,0:T(2,128)(2,1)} %bitcast.19, f32[3,4,128]{2,1,0:T(4,128)} %bitcast.12, bf16[4,2,3,3,128,128]{5,4,3,2,1,0:T(8,128)(2,1)} %history.1), custom_call_target="tpu_custom_call" | custom-call | tf_op jit(solution)/shard_map/terms/pallas_call | solution.py:312
  4.8 3.3 %collective-permute-start = (bf16[16,80,128]{2,1,0:T(8,128)(2,1)S(1)}, bf16[16,80,128]{2,1,0:T(8,128)(2,1)S(1)}, u32[]{:S(2)}, u32[]{:S(2)}) collective-permute-start(bf16[16,80,128]{2,1,0:T(8,128)(2,1)S(1)} %get-tuple-element.18), channel_id=1, source_target_pairs={{0,1},{1,0},{2,3},{3,2},{4,5},{5,4},{6,7},{7,6},{8,9},{9,8},{10,11... | collective-permute-start | bytes 983048 | tf_op jit(solution)/shard_map/ppermute | solution.py:328
  8.1 0.0 copy-done.3
  8.1 0.0 copy-done
  8.1 0.0 copy-done.4
  8.1 0.0 copy-done.5
  8.1 0.3 ahead.1
  8.5 0.9 %collective-permute-done.arrived = bf16[16,80,128]{2,1,0:T(8,128)(2,1)S(1)} collective-permute-done((bf16[16,80,128]{2,1,0:T(8,128)(2,1)S(1)}, bf16[16,80,128]{2,1,0:T(8,128)(2,1)S(1)}, u32[]{:S(2)}, u32[]{:S(2)}) %collective-permute-start) | collective-permute-done | bytes 327712 | tf_op jit(solution)/shard_map/ppermute | solution.py:328
  9.4 0.1 add_pair.1
  9.5 20.4 %all_to_all.10.arrived = bf16[16,80,128]{2,1,0:T(8,128)(2,1)S(1)} all-to-all(bf16[16,80,128]{2,1,0:T(8,128)(2,1)S(1)} %add_pair.1), channel_id=1, replica_groups={{0,2,4,6,8,10,12,14,16,18,20,22,24,26,28,30},{1,3,5,7,9,11,13,15,17,19,..., dimensions={0} | all-to-all | bytes 655360 | tf_op jit(solution)/shard_map/all_to_all | solution.py:357
  29.9 0.4 rows.1
  30.3 2.5 %collective-permute-start.1 = (bf16[16,2,384]{2,1,0:T(2,128)(2,1)S(1)}, bf16[16,2,384]{2,1,0:T(2,128)(2,1)S(1)}, u32[]{:S(2)}, u32[]{:S(2)}) collective-permute-start(bf16[16,2,384]{2,1,0:T(2,128)(2,1)S(1)} %get-tuple-element.25), channel_id=1, source_target_pairs={{0,1},{1,0},{2,3},{3,2},{4,5},{5,4},{6,7},{7,6},{8,9},{9,8},{10,11... | collective-permute-start | bytes 73736 | tf_op jit(solution)/shard_map/ppermute | solution.py:377
  32.8 0.6 %lattice.1 = (bf16[4,3,3,2,128]{4,3,2,1,0:T(2,128)(2,1)}, f32[1,128]{1,0:T(1,128)S(1)}) custom-call(f32[18,4,128]{2,1,0:T(4,128)S(1)} %get-tuple-element.22.fresh), custom_call_target="tpu_custom_call" | custom-call | flops 10000 | bytes 60000 | tf_op jit(solution)/shard_map/lattice/pallas_call | solution.py:378
  33.4 0.2 collective-permute-done.1.arrived
  33.6 0.1 add_shares.1
  33.7 21.3 %all_to_all.11.got = bf16[128,2,384]{2,1,0:T(2,128)(2,1)S(1)} all-to-all(bf16[128,2,384]{2,1,0:T(2,128)(2,1)S(1)} %bitcast.11), channel_id=1, replica_groups={{0,2,4,6,8,10,12,14,16,18,20,22,24,26,28,30,32,34,36,38,40,42,44,46,48,..., dimensions={0} | all-to-all | bytes 393216 | tf_op jit(solution)/shard_map/all_to_all | solution.py:401
  55.0 0.9 %finish.1 = (f32[3,3,2,4]{3,2,1,0:T(2,128)}, f32[2,4,64]{2,1,0:T(4,128)}) custom-call(bf16[128,2,384]{2,1,0:T(2,128)(2,1)S(1)} %all_to_all.11.got, f32[4,128]{1,0:T(4,128)S(1)} %get-tuple-element.19._.free), custom_call_target="tpu_custom_call" | custom-call | tf_op jit(solution)/shard_map/finish/pallas_call | solution.py:409
  (3 shorter events, 0.0 us)
Async XLA Ops:
  0.6 29.3 %copy-start.1 = (f32[4,3,128]{2,0,1:T(4,128)S(1)}, f32[4,3,128]{2,0,1:T(4,128)}, u32[]{:S(2)}) copy-start(f32[4,3,128]{2,0,1:T(4,128)} %param.11) | copy-start | bytes 18436
  0.6 7.5 %copy-start.3 = (f32[2,64,4]{1,2,0:T(4,128)S(1)}, f32[2,64,4]{1,2,0:T(4,128)}, u32[]{:S(2)}) copy-start(f32[2,64,4]{1,2,0:T(4,128)} %param.18) | copy-start | bytes 6148
  0.7 7.5 %copy-start = (bf16[4,2,64,128]{3,2,1,0:T(8,128)(2,1)S(1)}, bf16[4,2,64,128]{3,2,1,0:T(8,128)(2,1)}, u32[]{:S(2)}) copy-start(bf16[4,2,64,128]{3,2,1,0:T(8,128)(2,1)} %pseudo.1) | copy-start | bytes 393220
  0.7 7.5 %copy-start.4 = (s32[64,6]{0,1:T(8,128)S(1)}, s32[64,6]{0,1:T(8,128)}, u32[]{:S(2)}) copy-start(s32[64,6]{0,1:T(8,128)} %param.17) | copy-start | bytes 4612
  0.7 7.4 %copy-start.5 = (f32[64]{0:T(128)S(1)}, f32[64]{0:T(128)}, u32[]{:S(2)}) copy-start(f32[64]{0:T(128)} %param.16) | copy-start | bytes 772
  0.7 29.2 %copy-start.2 = (f32[2,3,3,128]{3,0,2,1:T(2,128)S(1)}, f32[2,3,3,128]{3,0,2,1:T(2,128)}, u32[]{:S(2)}) copy-start(f32[2,3,3,128]{3,0,2,1:T(2,128)} %param.14) | copy-start | bytes 27652
  0.7 29.2 %copy-start.6 = (s32[128]{0:T(128)S(1)}, s32[128]{0:T(128)}, u32[]{:S(2)}) copy-start(s32[128]{0:T(128)} %param.15) | copy-start | bytes 1540
  4.8 4.6 %collective-permute-start = (bf16[16,80,128]{2,1,0:T(8,128)(2,1)S(1)}, bf16[16,80,128]{2,1,0:T(8,128)(2,1)S(1)}, u32[]{:S(2)}, u32[]{:S(2)}) collective-permute-start(bf16[16,80,128]{2,1,0:T(8,128)(2,1)S(1)} %get-tuple-element.18), channel_id=1, source_target_pairs={{0,1},{1,0},{2,3},{3,2},{4,5},{5,4},{6,7},{7,6},{8,9},{9,8},{10,11... | collective-permute-start | bytes 983048 | tf_op jit(solution)/shard_map/ppermute | solution.py:328
  30.3 3.4 %collective-permute-start.1 = (bf16[16,2,384]{2,1,0:T(2,128)(2,1)S(1)}, bf16[16,2,384]{2,1,0:T(2,128)(2,1)S(1)}, u32[]{:S(2)}, u32[]{:S(2)}) collective-permute-start(bf16[16,2,384]{2,1,0:T(2,128)(2,1)S(1)} %get-tuple-element.25), channel_id=1, source_target_pairs={{0,1},{1,0},{2,3},{3,2},{4,5},{5,4},{6,7},{7,6},{8,9},{9,8},{10,11... | collective-permute-start | bytes 73736 | tf_op jit(solution)/shard_map/ppermute | solution.py:377

commit v4 on v3

--- a/solution.py
+++ b/solution.py
@@ -12,6 +12,18 @@
 HIGHEST = lax.Precision.HIGHEST
 TERMS = 80
 CHUNKS = 4
+
+
+def slot_of(chip, chips):
+    half = chips // 2
+    return lax.rem(chip, half) * 2 + lax.div(chip, half)
+
+
+def spread(chips):
+    half = chips // 2
+    bits = half.bit_length() - 1
+    order = [sum((i >> b & 1) << (bits - 1 - b) for b in range(bits)) for i in range(half)]
+    return [h * half + i for i in order for h in range(2)]
 
 
 def flag(condition):
@@ -111,8 +123,9 @@
             odds.append(energies * flag(position > 2 * chip + 1))
             even = jnp.concatenate(evens, axis=0).astype(BF16)
             odd = jnp.concatenate(odds, axis=0).astype(BF16)
-            own[chip] = jnp.where(even_core, even, odd)
-            other[chip] = jnp.where(even_core, odd, even)
+            slot = slot_of(chip, own.shape[0])
+            own[slot] = jnp.where(even_core, even, odd)
+            other[slot] = jnp.where(even_core, odd, even)
 
     @pl.loop(0, CHUNKS)
     def _(i):
@@ -235,10 +248,10 @@
 
 
 def add_shares_kernel(own, arrived, _, out):
-    for t in range(own.shape[0]):
+    for i, t in enumerate(spread(own.shape[0])):
         tile = (own[t].astype(F32) + arrived[t].astype(F32)).astype(BF16)
-        for k in range(out.shape[0]):
-            out[k, t] = tile
+        for k in range(out.shape[1]):
+            out[i, k] = tile
 
 
 def lattice_kernel(fresh, lattice, written):
@@ -353,7 +366,8 @@
         compiler_params=grant(8),
         name="add_pair",
     )(own, swapped, free)
-    same_core = [[2 * t + c for t in range(chips)] for c in range(2)]
+    half = chips // 2
+    same_core = [[2 * (h * half + i) + c for i in range(half) for h in range(2)] for c in range(2)]
     arrived = lax.all_to_all(
         paired, "hist", split_axis=0, concat_axis=0, tiled=True, axis_index_groups=same_core
     )
@@ -389,14 +403,14 @@
     )(fresh)
     paired = pl.pallas_call(
         add_shares_kernel,
-        out_shape=jax.ShapeDtypeStruct((ka_size, *shares.shape), BF16),
+        out_shape=jax.ShapeDtypeStruct((chips, ka_size, *shares.shape[1:]), BF16),
         in_specs=[VMEM, VMEM, ANY],
         out_specs=VMEM,
         compiler_params=grant(8),
         name="add_shares",
     )(own, swapped, written)
     same_core = [
-        [k * hist_size + 2 * t + c for k in range(ka_size) for t in range(chips)] for c in range(2)
+        [k * hist_size + 2 * t + c for t in spread(chips) for k in range(ka_size)] for c in range(2)
     ]
     got = lax.all_to_all(
         paired.reshape(ka_size * chips, 2, 3 * lanes),

time: 56 us -> 55.1 us (0.984); the launches traced: 55.8 us -> 54.1 us
  blocking collectives: 41.7 us -> 40.6 us
  starting transfers between devices: 5.83 us -> 5.23 us
    all_to_all x1, blocking collectives: 21.3 us -> 17.8 us  [per_device(): lax.all_to_all(paired.reshape(ka_size * chips, 2, 3 * lanes), ('ka', 'his...]
    all_to_all x1, blocking collectives: 20.4 us -> 22.8 us  [per_device(): lax.all_to_all(paired, 'hist', split_axis=0, concat_axis=0, tiled=True, a...]
    ppermute x2, starting transfers between devices: 5.83 us -> 5.23 us  [per_device(): swapped = lax.ppermute(other, 'hist', cores)]
where the time goes in v4:
time: 55.1 us; the launch traced here: 54.1 us
  blocking collectives  40.6 us (74%)
  Pallas kernels  5.65 us (10%)
  starting transfers between devices  5.23 us (9%)
  between operations  1.43 us (3%)
  waiting for transfers between devices  1.13 us (2%)
    all_to_all x1, blocking collectives, per_device(): lax.all_to_all(paired, 'hist', split_axis=0, concat_axis=0, tiled=True, a...  22.8 us
    all_to_all x1, blocking collectives, per_device(): lax.all_to_all(paired.reshape(ka_size * chips, 2, 3 * lanes), ('ka', 'his...  17.8 us
    ppermute x2, starting transfers between devices, per_device(): swapped = lax.ppermute(other, 'hist', cores)  5.23 us
    pallas_call x1, Pallas kernels, per_device(): pl.pallas_call(terms_kernel, out_shape=(tiles, tiles, jax.ShapeDtypeStruc...  3.24 us
    ppermute x2, waiting for transfers between devices, per_device(): swapped = lax.ppermute(other, 'hist', cores)  1.13 us
  transfers between devices with their start and end apart: 2, of which 2 were waited for; matrix products, arithmetic and copies ran while one was open for 0% of the time, Pallas kernels for 2%

profile of v4, /device:TPU:1, one launch (start us, length us, event | category | flops | bytes accessed | tf_op | source)
XLA Modules:
  0.0 54.1 jit_solution(6628550610395356483)
XLA Ops:
  0.6 0.0 copy-start.1
  0.6 0.0 copy-start.3
  0.7 0.0 copy-start
  0.7 0.0 copy-start.4
  0.7 0.0 copy-start.5
  0.7 0.0 copy-start.2
  0.7 0.0 copy-start.6
  1.4 3.2 %terms.1 = (bf16[16,80,128]{2,1,0:T(8,128)(2,1)S(1)}, bf16[16,80,128]{2,1,0:T(8,128)(2,1)S(1)}, s32[1,128]{1,0:T(1,128)S(1)}) custom-call(s32[1]{0:T(128)S(6)} %copy.13.step, bf16[4,3,3,2,128]{4,3,2,1,0:T(2,128)(2,1)} %bitcast.19, f32[3,4,128]{2,1,0:T(4,128)} %bitcast.12, bf16[4,2,3,3,128,128]{5,4,3,2,1,0:T(8,128)(2,1)} %history.1), custom_call_target="tpu_custom_call" | custom-call | tf_op jit(solution)/shard_map/terms/pallas_call | solution.py:325
  4.7 3.3 %collective-permute-start = (bf16[16,80,128]{2,1,0:T(8,128)(2,1)S(1)}, bf16[16,80,128]{2,1,0:T(8,128)(2,1)S(1)}, u32[]{:S(2)}, u32[]{:S(2)}) collective-permute-start(bf16[16,80,128]{2,1,0:T(8,128)(2,1)S(1)} %get-tuple-element.18), channel_id=1, source_target_pairs={{0,1},{1,0},{2,3},{3,2},{4,5},{5,4},{6,7},{7,6},{8,9},{9,8},{10,11... | collective-permute-start | bytes 983048 | tf_op jit(solution)/shard_map/ppermute | solution.py:341
  8.0 0.0 copy-done.3
  8.0 0.0 copy-done
  8.0 0.0 copy-done.4
  8.0 0.3 ahead.1
  8.3 0.9 %collective-permute-done.arrived = bf16[16,80,128]{2,1,0:T(8,128)(2,1)S(1)} collective-permute-done((bf16[16,80,128]{2,1,0:T(8,128)(2,1)S(1)}, bf16[16,80,128]{2,1,0:T(8,128)(2,1)S(1)}, u32[]{:S(2)}, u32[]{:S(2)}) %collective-permute-start) | collective-permute-done | bytes 327712 | tf_op jit(solution)/shard_map/ppermute | solution.py:341
  9.2 0.1 add_pair.1
  9.4 22.8 %all_to_all.10.arrived = bf16[16,80,128]{2,1,0:T(8,128)(2,1)S(1)} all-to-all(bf16[16,80,128]{2,1,0:T(8,128)(2,1)S(1)} %add_pair.1), channel_id=1, replica_groups={{0,16,2,18,4,20,6,22,8,24,10,26,12,28,14,30},{1,17,3,19,5,21,7,23,9,25,..., dimensions={0} | all-to-all | bytes 655360 | tf_op jit(solution)/shard_map/all_to_all | solution.py:371
  32.2 0.0 copy-done.6
  32.2 0.4 rows.1
  32.6 1.9 %collective-permute-start.1 = (bf16[16,2,384]{2,1,0:T(2,128)(2,1)S(1)}, bf16[16,2,384]{2,1,0:T(2,128)(2,1)S(1)}, u32[]{:S(2)}, u32[]{:S(2)}) collective-permute-start(bf16[16,2,384]{2,1,0:T(2,128)(2,1)S(1)} %get-tuple-element.25), channel_id=1, source_target_pairs={{0,1},{1,0},{2,3},{3,2},{4,5},{5,4},{6,7},{7,6},{8,9},{9,8},{10,11... | collective-permute-start | bytes 73736 | tf_op jit(solution)/shard_map/ppermute | solution.py:391
  34.5 0.6 %lattice.1 = (bf16[4,3,3,2,128]{4,3,2,1,0:T(2,128)(2,1)}, f32[1,128]{1,0:T(1,128)S(1)}) custom-call(f32[18,4,128]{2,1,0:T(4,128)S(1)} %get-tuple-element.22.fresh), custom_call_target="tpu_custom_call" | custom-call | flops 10000 | bytes 60000 | tf_op jit(solution)/shard_map/lattice/pallas_call | solution.py:392
  35.1 0.2 collective-permute-done.1.arrived
  35.4 0.1 add_shares.1
  35.4 17.8 %all_to_all.11.got = bf16[128,2,384]{2,1,0:T(2,128)(2,1)S(1)} all-to-all(bf16[128,2,384]{2,1,0:T(2,128)(2,1)S(1)} %bitcast.11), channel_id=1, replica_groups={{0,32,64,96,128,160,192,224,16,48,80,112,144,176,208,240,8,40,72,104,13..., dimensions={0} | all-to-all | bytes 393216 | tf_op jit(solution)/shard_map/all_to_all | solution.py:415
  53.2 0.9 %finish.1 = (f32[3,3,2,4]{3,2,1,0:T(2,128)}, f32[2,4,64]{2,1,0:T(4,128)}) custom-call(bf16[128,2,384]{2,1,0:T(2,128)(2,1)S(1)} %all_to_all.11.got, f32[4,128]{1,0:T(4,128)S(1)} %get-tuple-element.19._.free), custom_call_target="tpu_custom_call" | custom-call | tf_op jit(solution)/shard_map/finish/pallas_call | solution.py:423
  (3 shorter events, 0.0 us)
Async XLA Ops:
  0.6 31.6 %copy-start.1 = (f32[4,3,128]{2,0,1:T(4,128)S(1)}, f32[4,3,128]{2,0,1:T(4,128)}, u32[]{:S(2)}) copy-start(f32[4,3,128]{2,0,1:T(4,128)} %param.11) | copy-start | bytes 18436
  0.6 7.3 %copy-start.3 = (f32[2,64,4]{1,2,0:T(4,128)S(1)}, f32[2,64,4]{1,2,0:T(4,128)}, u32[]{:S(2)}) copy-start(f32[2,64,4]{1,2,0:T(4,128)} %param.18) | copy-start | bytes 6148
  0.7 7.3 %copy-start = (bf16[4,2,64,128]{3,2,1,0:T(8,128)(2,1)S(1)}, bf16[4,2,64,128]{3,2,1,0:T(8,128)(2,1)}, u32[]{:S(2)}) copy-start(bf16[4,2,64,128]{3,2,1,0:T(8,128)(2,1)} %pseudo.1) | copy-start | bytes 393220
  0.7 7.3 %copy-start.4 = (s32[64,6]{0,1:T(8,128)S(1)}, s32[64,6]{0,1:T(8,128)}, u32[]{:S(2)}) copy-start(s32[64,6]{0,1:T(8,128)} %param.17) | copy-start | bytes 4612
  0.7 7.3 %copy-start.5 = (f32[64]{0:T(128)S(1)}, f32[64]{0:T(128)}, u32[]{:S(2)}) copy-start(f32[64]{0:T(128)} %param.16) | copy-start | bytes 772
  0.7 31.5 %copy-start.2 = (f32[2,3,3,128]{3,0,2,1:T(2,128)S(1)}, f32[2,3,3,128]{3,0,2,1:T(2,128)}, u32[]{:S(2)}) copy-start(f32[2,3,3,128]{3,0,2,1:T(2,128)} %param.14) | copy-start | bytes 27652
  0.7 31.5 %copy-start.6 = (s32[128]{0:T(128)S(1)}, s32[128]{0:T(128)}, u32[]{:S(2)}) copy-start(s32[128]{0:T(128)} %param.15) | copy-start | bytes 1540
  4.7 4.6 %collective-permute-start = (bf16[16,80,128]{2,1,0:T(8,128)(2,1)S(1)}, bf16[16,80,128]{2,1,0:T(8,128)(2,1)S(1)}, u32[]{:S(2)}, u32[]{:S(2)}) collective-permute-start(bf16[16,80,128]{2,1,0:T(8,128)(2,1)S(1)} %get-tuple-element.18), channel_id=1, source_target_pairs={{0,1},{1,0},{2,3},{3,2},{4,5},{5,4},{6,7},{7,6},{8,9},{9,8},{10,11... | collective-permute-start | bytes 983048 | tf_op jit(solution)/shard_map/ppermute | solution.py:341
  32.6 2.8 %collective-permute-start.1 = (bf16[16,2,384]{2,1,0:T(2,128)(2,1)S(1)}, bf16[16,2,384]{2,1,0:T(2,128)(2,1)S(1)}, u32[]{:S(2)}, u32[]{:S(2)}) collective-permute-start(bf16[16,2,384]{2,1,0:T(2,128)(2,1)S(1)} %get-tuple-element.25), channel_id=1, source_target_pairs={{0,1},{1,0},{2,3},{3,2},{4,5},{5,4},{6,7},{7,6},{8,9},{9,8},{10,11... | collective-permute-start | bytes 73736 | tf_op jit(solution)/shard_map/ppermute | solution.py:391

commit v5 on v4

--- a/solution.py
+++ b/solution.py
@@ -19,11 +19,15 @@
     return lax.rem(chip, half) * 2 + lax.div(chip, half)
 
 
+def alternate(order):
+    return [h * len(order) + i for i in order for h in range(2)]
+
+
 def spread(chips):
     half = chips // 2
     bits = half.bit_length() - 1
     order = [sum((i >> b & 1) << (bits - 1 - b) for b in range(bits)) for i in range(half)]
-    return [h * half + i for i in order for h in range(2)]
+    return alternate(order)
 
 
 def flag(condition):
@@ -366,8 +370,7 @@
         compiler_params=grant(8),
         name="add_pair",
     )(own, swapped, free)
-    half = chips // 2
-    same_core = [[2 * (h * half + i) + c for i in range(half) for h in range(2)] for c in range(2)]
+    same_core = [[2 * t + c for t in alternate(range(chips // 2))] for c in range(2)]
     arrived = lax.all_to_all(
         paired, "hist", split_axis=0, concat_axis=0, tiled=True, axis_index_groups=same_core
     )
@@ -410,7 +413,8 @@
         name="add_shares",
     )(own, swapped, written)
     same_core = [
-        [k * hist_size + 2 * t + c for t in spread(chips) for k in range(ka_size)] for c in range(2)
+        [k * hist_size + 2 * t + c for t in spread(chips) for k in alternate(range(ka_size // 2))]
+        for c in range(2)
     ]
     got = lax.all_to_all(
         paired.reshape(ka_size * chips, 2, 3 * lanes),

time: 55.1 us -> 54.7 us (level)
  no operation moved by 1% of the time
where the time goes in v5:
time: 54.7 us; the launch traced here: 53.8 us
  blocking collectives  40.4 us (74%)
  Pallas kernels  5.65 us (10%)
  starting transfers between devices  5.23 us (10%)
  between operations  1.43 us (3%)
  waiting for transfers between devices  1.13 us (2%)
    all_to_all x1, blocking collectives, per_device(): lax.all_to_all(paired, 'hist', split_axis=0, concat_axis=0, tiled=True, a...  22.8 us
    all_to_all x1, blocking collectives, per_device(): lax.all_to_all(paired.reshape(ka_size * chips, 2, 3 * lanes), ('ka', 'his...  17.5 us
    ppermute x2, starting transfers between devices, per_device(): swapped = lax.ppermute(other, 'hist', cores)  5.23 us
    pallas_call x1, Pallas kernels, per_device(): pl.pallas_call(terms_kernel, out_shape=(tiles, tiles, jax.ShapeDtypeStruc...  3.24 us
    ppermute x2, waiting for transfers between devices, per_device(): swapped = lax.ppermute(other, 'hist', cores)  1.13 us
  transfers between devices with their start and end apart: 2, of which 2 were waited for; matrix products, arithmetic and copies ran while one was open for 0% of the time, Pallas kernels for 2%

profile of v5, /device:TPU:1, one launch (start us, length us, event | category | flops | bytes accessed | tf_op | source)
XLA Modules:
  0.0 53.8 jit_solution(15784578231566273475)
XLA Ops:
  0.6 0.0 copy-start.1
  0.6 0.0 copy-start.3
  0.7 0.0 copy-start
  0.7 0.0 copy-start.4
  0.7 0.0 copy-start.5
  0.7 0.0 copy-start.2
  0.7 0.0 copy-start.6
  1.4 3.2 %terms.1 = (bf16[16,80,128]{2,1,0:T(8,128)(2,1)S(1)}, bf16[16,80,128]{2,1,0:T(8,128)(2,1)S(1)}, s32[1,128]{1,0:T(1,128)S(1)}) custom-call(s32[1]{0:T(128)S(6)} %copy.13.step, bf16[4,3,3,2,128]{4,3,2,1,0:T(2,128)(2,1)} %bitcast.19, f32[3,4,128]{2,1,0:T(4,128)} %bitcast.12, bf16[4,2,3,3,128,128]{5,4,3,2,1,0:T(8,128)(2,1)} %history.1), custom_call_target="tpu_custom_call" | custom-call | tf_op jit(solution)/shard_map/terms/pallas_call | solution.py:329
  4.7 3.3 %collective-permute-start = (bf16[16,80,128]{2,1,0:T(8,128)(2,1)S(1)}, bf16[16,80,128]{2,1,0:T(8,128)(2,1)S(1)}, u32[]{:S(2)}, u32[]{:S(2)}) collective-permute-start(bf16[16,80,128]{2,1,0:T(8,128)(2,1)S(1)} %get-tuple-element.18), channel_id=1, source_target_pairs={{0,1},{1,0},{2,3},{3,2},{4,5},{5,4},{6,7},{7,6},{8,9},{9,8},{10,11... | collective-permute-start | bytes 983048 | tf_op jit(solution)/shard_map/ppermute | solution.py:345
  8.0 0.0 copy-done.3
  8.0 0.0 copy-done
  8.0 0.0 copy-done.4
  8.0 0.0 copy-done.5
  8.0 0.3 ahead.1
  8.3 0.9 %collective-permute-done.arrived = bf16[16,80,128]{2,1,0:T(8,128)(2,1)S(1)} collective-permute-done((bf16[16,80,128]{2,1,0:T(8,128)(2,1)S(1)}, bf16[16,80,128]{2,1,0:T(8,128)(2,1)S(1)}, u32[]{:S(2)}, u32[]{:S(2)}) %collective-permute-start) | collective-permute-done | bytes 327712 | tf_op jit(solution)/shard_map/ppermute | solution.py:345
  9.2 0.1 add_pair.1
  9.4 22.8 %all_to_all.10.arrived = bf16[16,80,128]{2,1,0:T(8,128)(2,1)S(1)} all-to-all(bf16[16,80,128]{2,1,0:T(8,128)(2,1)S(1)} %add_pair.1), channel_id=1, replica_groups={{0,16,2,18,4,20,6,22,8,24,10,26,12,28,14,30},{1,17,3,19,5,21,7,23,9,25,..., dimensions={0} | all-to-all | bytes 655360 | tf_op jit(solution)/shard_map/all_to_all | solution.py:374
  32.2 0.4 rows.1
  32.6 1.9 %collective-permute-start.1 = (bf16[16,2,384]{2,1,0:T(2,128)(2,1)S(1)}, bf16[16,2,384]{2,1,0:T(2,128)(2,1)S(1)}, u32[]{:S(2)}, u32[]{:S(2)}) collective-permute-start(bf16[16,2,384]{2,1,0:T(2,128)(2,1)S(1)} %get-tuple-element.25), channel_id=1, source_target_pairs={{0,1},{1,0},{2,3},{3,2},{4,5},{5,4},{6,7},{7,6},{8,9},{9,8},{10,11... | collective-permute-start | bytes 73736 | tf_op jit(solution)/shard_map/ppermute | solution.py:394
  34.5 0.6 %lattice.1 = (bf16[4,3,3,2,128]{4,3,2,1,0:T(2,128)(2,1)}, f32[1,128]{1,0:T(1,128)S(1)}) custom-call(f32[18,4,128]{2,1,0:T(4,128)S(1)} %get-tuple-element.22.fresh), custom_call_target="tpu_custom_call" | custom-call | flops 10000 | bytes 60000 | tf_op jit(solution)/shard_map/lattice/pallas_call | solution.py:395
  35.1 0.2 collective-permute-done.1.arrived
  35.4 0.1 add_shares.1
  35.4 17.5 %all_to_all.11.got = bf16[128,2,384]{2,1,0:T(2,128)(2,1)S(1)} all-to-all(bf16[128,2,384]{2,1,0:T(2,128)(2,1)S(1)} %bitcast.11), channel_id=1, replica_groups={{0,128,32,160,64,192,96,224,16,144,48,176,80,208,112,240,8,136,40,168,7..., dimensions={0} | all-to-all | bytes 393216 | tf_op jit(solution)/shard_map/all_to_all | solution.py:419
  53.0 0.9 %finish.1 = (f32[3,3,2,4]{3,2,1,0:T(2,128)}, f32[2,4,64]{2,1,0:T(4,128)}) custom-call(bf16[128,2,384]{2,1,0:T(2,128)(2,1)S(1)} %all_to_all.11.got, f32[4,128]{1,0:T(4,128)S(1)} %get-tuple-element.19._.free), custom_call_target="tpu_custom_call" | custom-call | tf_op jit(solution)/shard_map/finish/pallas_call | solution.py:427
  (3 shorter events, 0.0 us)
Async XLA Ops:
  0.6 31.6 %copy-start.1 = (f32[4,3,128]{2,0,1:T(4,128)S(1)}, f32[4,3,128]{2,0,1:T(4,128)}, u32[]{:S(2)}) copy-start(f32[4,3,128]{2,0,1:T(4,128)} %param.11) | copy-start | bytes 18436
  0.6 7.3 %copy-start.3 = (f32[2,64,4]{1,2,0:T(4,128)S(1)}, f32[2,64,4]{1,2,0:T(4,128)}, u32[]{:S(2)}) copy-start(f32[2,64,4]{1,2,0:T(4,128)} %param.18) | copy-start | bytes 6148
  0.7 7.3 %copy-start = (bf16[4,2,64,128]{3,2,1,0:T(8,128)(2,1)S(1)}, bf16[4,2,64,128]{3,2,1,0:T(8,128)(2,1)}, u32[]{:S(2)}) copy-start(bf16[4,2,64,128]{3,2,1,0:T(8,128)(2,1)} %pseudo.1) | copy-start | bytes 393220
  0.7 7.3 %copy-start.4 = (s32[64,6]{0,1:T(8,128)S(1)}, s32[64,6]{0,1:T(8,128)}, u32[]{:S(2)}) copy-start(s32[64,6]{0,1:T(8,128)} %param.17) | copy-start | bytes 4612
  0.7 7.3 %copy-start.5 = (f32[64]{0:T(128)S(1)}, f32[64]{0:T(128)}, u32[]{:S(2)}) copy-start(f32[64]{0:T(128)} %param.16) | copy-start | bytes 772
  0.7 31.5 %copy-start.2 = (f32[2,3,3,128]{3,0,2,1:T(2,128)S(1)}, f32[2,3,3,128]{3,0,2,1:T(2,128)}, u32[]{:S(2)}) copy-start(f32[2,3,3,128]{3,0,2,1:T(2,128)} %param.14) | copy-start | bytes 27652
  0.7 31.5 %copy-start.6 = (s32[128]{0:T(128)S(1)}, s32[128]{0:T(128)}, u32[]{:S(2)}) copy-start(s32[128]{0:T(128)} %param.15) | copy-start | bytes 1540
  4.7 4.6 %collective-permute-start = (bf16[16,80,128]{2,1,0:T(8,128)(2,1)S(1)}, bf16[16,80,128]{2,1,0:T(8,128)(2,1)S(1)}, u32[]{:S(2)}, u32[]{:S(2)}) collective-permute-start(bf16[16,80,128]{2,1,0:T(8,128)(2,1)S(1)} %get-tuple-element.18), channel_id=1, source_target_pairs={{0,1},{1,0},{2,3},{3,2},{4,5},{5,4},{6,7},{7,6},{8,9},{9,8},{10,11... | collective-permute-start | bytes 983048 | tf_op jit(solution)/shard_map/ppermute | solution.py:345
  32.6 2.8 %collective-permute-start.1 = (bf16[16,2,384]{2,1,0:T(2,128)(2,1)S(1)}, bf16[16,2,384]{2,1,0:T(2,128)(2,1)S(1)}, u32[]{:S(2)}, u32[]{:S(2)}) collective-permute-start(bf16[16,2,384]{2,1,0:T(2,128)(2,1)S(1)} %get-tuple-element.25), channel_id=1, source_target_pairs={{0,1},{1,0},{2,3},{3,2},{4,5},{5,4},{6,7},{7,6},{8,9},{9,8},{10,11... | collective-permute-start | bytes 73736 | tf_op jit(solution)/shard_map/ppermute | solution.py:394

commit v6 on v5

--- a/solution.py
+++ b/solution.py
@@ -11,7 +11,7 @@
 BF16 = jnp.bfloat16
 HIGHEST = lax.Precision.HIGHEST
 TERMS = 80
-CHUNKS = 4
+CHUNKS = 8
 
 
 def slot_of(chip, chips):
@@ -66,7 +66,7 @@
     ]
     for copy in small:
         copy.start()
-    for i in range(CHUNKS):
+    for i in range(4):
         fetch(i).start()
     for copy in small:
         copy.wait()
@@ -134,6 +134,10 @@
     @pl.loop(0, CHUNKS)
     def _(i):
         fetch(i).wait()
+
+        @pl.when(i + 4 < CHUNKS)
+        def _():
+            fetch(i + 4).start()
 
         @pl.loop(0, wide // 16)
         def _(h):
@@ -282,10 +286,11 @@
     sums = total[0:1, 2 * lanes :] + total[1:2, 2 * lanes :]
     count = sums[:, 72:73]
     mean = sums / count
+    pair = jnp.concatenate([mean, pltpu.roll(mean, lanes - 4, 1)], axis=0)
     for a in range(3):
         for c in range(3):
             i = (a * 3 + c) * 8
-            local[a, c] = jnp.concatenate([mean[:, i : i + 4], mean[:, i + 4 : i + 8]], axis=0)
+            local[a, c] = pair[:, i : i + 4]
     shares = jnp.concatenate([total[:, :lanes], total[:, lanes : 2 * lanes]], axis=0)
     out = free[...] + shares / count
     pseudo[0] = out[:, :states]

time: 54.7 us -> 54.7 us (level)
  no operation moved by 1% of the time
where the time goes in v6:
time: 54.7 us; the launch traced here: 53.7 us
  blocking collectives  40.4 us (74%)
  Pallas kernels  5.54 us (10%)
  starting transfers between devices  5.23 us (10%)
  between operations  1.43 us (3%)
  waiting for transfers between devices  1.13 us (2%)
    all_to_all x1, blocking collectives, per_device(): lax.all_to_all(paired, 'hist', split_axis=0, concat_axis=0, tiled=True, a...  22.8 us
    all_to_all x1, blocking collectives, per_device(): lax.all_to_all(paired.reshape(ka_size * chips, 2, 3 * lanes), ('ka', 'his...  17.5 us
    ppermute x2, starting transfers between devices, per_device(): swapped = lax.ppermute(other, 'hist', cores)  5.23 us
    pallas_call x1, Pallas kernels, per_device(): pl.pallas_call(terms_kernel, out_shape=(tiles, tiles, jax.ShapeDtypeStruc...  3.13 us
    ppermute x2, waiting for transfers between devices, per_device(): swapped = lax.ppermute(other, 'hist', cores)  1.13 us
  transfers between devices with their start and end apart: 2, of which 2 were waited for; matrix products, arithmetic and copies ran while one was open for 0% of the time, Pallas kernels for 2%

profile of v6, /device:TPU:1, one launch (start us, length us, event | category | flops | bytes accessed | tf_op | source)
XLA Modules:
  0.0 53.7 jit_solution(13109087025241322964)
XLA Ops:
  0.6 0.0 copy-start.1
  0.6 0.0 copy-start.3
  0.7 0.0 copy-start
  0.7 0.0 copy-start.4
  0.7 0.0 copy-start.5
  0.7 0.0 copy-start.2
  0.7 0.0 copy-start.6
  1.4 3.1 %terms.1 = (bf16[16,80,128]{2,1,0:T(8,128)(2,1)S(1)}, bf16[16,80,128]{2,1,0:T(8,128)(2,1)S(1)}, s32[1,128]{1,0:T(1,128)S(1)}) custom-call(s32[1]{0:T(128)S(6)} %copy.13.step, bf16[4,3,3,2,128]{4,3,2,1,0:T(2,128)(2,1)} %bitcast.19, f32[3,4,128]{2,1,0:T(4,128)} %bitcast.12, bf16[4,2,3,3,128,128]{5,4,3,2,1,0:T(8,128)(2,1)} %history.1), custom_call_target="tpu_custom_call" | custom-call | tf_op jit(solution)/shard_map/terms/pallas_call | solution.py:334
  4.5 3.3 %collective-permute-start = (bf16[16,80,128]{2,1,0:T(8,128)(2,1)S(1)}, bf16[16,80,128]{2,1,0:T(8,128)(2,1)S(1)}, u32[]{:S(2)}, u32[]{:S(2)}) collective-permute-start(bf16[16,80,128]{2,1,0:T(8,128)(2,1)S(1)} %get-tuple-element.18), channel_id=1, source_target_pairs={{0,1},{1,0},{2,3},{3,2},{4,5},{5,4},{6,7},{7,6},{8,9},{9,8},{10,11... | collective-permute-start | bytes 983048 | tf_op jit(solution)/shard_map/ppermute | solution.py:350
  7.9 0.0 copy-done.3
  7.9 0.0 copy-done
  7.9 0.0 copy-done.4
  7.9 0.0 copy-done.5
  7.9 0.3 ahead.1
  8.2 0.9 %collective-permute-done.arrived = bf16[16,80,128]{2,1,0:T(8,128)(2,1)S(1)} collective-permute-done((bf16[16,80,128]{2,1,0:T(8,128)(2,1)S(1)}, bf16[16,80,128]{2,1,0:T(8,128)(2,1)S(1)}, u32[]{:S(2)}, u32[]{:S(2)}) %collective-permute-start) | collective-permute-done | bytes 327712 | tf_op jit(solution)/shard_map/ppermute | solution.py:350
  9.1 0.1 add_pair.1
  9.3 22.8 %all_to_all.10.arrived = bf16[16,80,128]{2,1,0:T(8,128)(2,1)S(1)} all-to-all(bf16[16,80,128]{2,1,0:T(8,128)(2,1)S(1)} %add_pair.1), channel_id=1, replica_groups={{0,16,2,18,4,20,6,22,8,24,10,26,12,28,14,30},{1,17,3,19,5,21,7,23,9,25,..., dimensions={0} | all-to-all | bytes 655360 | tf_op jit(solution)/shard_map/all_to_all | solution.py:379
  32.1 0.4 rows.1
  32.5 1.9 %collective-permute-start.1 = (bf16[16,2,384]{2,1,0:T(2,128)(2,1)S(1)}, bf16[16,2,384]{2,1,0:T(2,128)(2,1)S(1)}, u32[]{:S(2)}, u32[]{:S(2)}) collective-permute-start(bf16[16,2,384]{2,1,0:T(2,128)(2,1)S(1)} %get-tuple-element.25), channel_id=1, source_target_pairs={{0,1},{1,0},{2,3},{3,2},{4,5},{5,4},{6,7},{7,6},{8,9},{9,8},{10,11... | collective-permute-start | bytes 73736 | tf_op jit(solution)/shard_map/ppermute | solution.py:399
  34.4 0.6 %lattice.1 = (bf16[4,3,3,2,128]{4,3,2,1,0:T(2,128)(2,1)}, f32[1,128]{1,0:T(1,128)S(1)}) custom-call(f32[18,4,128]{2,1,0:T(4,128)S(1)} %get-tuple-element.22.fresh), custom_call_target="tpu_custom_call" | custom-call | flops 10000 | bytes 60000 | tf_op jit(solution)/shard_map/lattice/pallas_call | solution.py:400
  35.0 0.2 collective-permute-done.1.arrived
  35.2 0.1 add_shares.1
  35.3 17.5 %all_to_all.11.got = bf16[128,2,384]{2,1,0:T(2,128)(2,1)S(1)} all-to-all(bf16[128,2,384]{2,1,0:T(2,128)(2,1)S(1)} %bitcast.11), channel_id=1, replica_groups={{0,128,32,160,64,192,96,224,16,144,48,176,80,208,112,240,8,136,40,168,7..., dimensions={0} | all-to-all | bytes 393216 | tf_op jit(solution)/shard_map/all_to_all | solution.py:424
  52.9 0.9 %finish.1 = (f32[3,3,2,4]{3,2,1,0:T(2,128)}, f32[2,4,64]{2,1,0:T(4,128)}) custom-call(bf16[128,2,384]{2,1,0:T(2,128)(2,1)S(1)} %all_to_all.11.got, f32[4,128]{1,0:T(4,128)S(1)} %get-tuple-element.19._.free), custom_call_target="tpu_custom_call" | custom-call | tf_op jit(solution)/shard_map/finish/pallas_call | solution.py:432
  (3 shorter events, 0.0 us)
Async XLA Ops:
  0.6 31.5 %copy-start.1 = (f32[4,3,128]{2,0,1:T(4,128)S(1)}, f32[4,3,128]{2,0,1:T(4,128)}, u32[]{:S(2)}) copy-start(f32[4,3,128]{2,0,1:T(4,128)} %param.11) | copy-start | bytes 18436
  0.6 7.2 %copy-start.3 = (f32[2,64,4]{1,2,0:T(4,128)S(1)}, f32[2,64,4]{1,2,0:T(4,128)}, u32[]{:S(2)}) copy-start(f32[2,64,4]{1,2,0:T(4,128)} %param.18) | copy-start | bytes 6148
  0.7 7.2 %copy-start = (bf16[4,2,64,128]{3,2,1,0:T(8,128)(2,1)S(1)}, bf16[4,2,64,128]{3,2,1,0:T(8,128)(2,1)}, u32[]{:S(2)}) copy-start(bf16[4,2,64,128]{3,2,1,0:T(8,128)(2,1)} %pseudo.1) | copy-start | bytes 393220
  0.7 7.2 %copy-start.4 = (s32[64,6]{0,1:T(8,128)S(1)}, s32[64,6]{0,1:T(8,128)}, u32[]{:S(2)}) copy-start(s32[64,6]{0,1:T(8,128)} %param.17) | copy-start | bytes 4612
  0.7 7.2 %copy-start.5 = (f32[64]{0:T(128)S(1)}, f32[64]{0:T(128)}, u32[]{:S(2)}) copy-start(f32[64]{0:T(128)} %param.16) | copy-start | bytes 772
  0.7 31.4 %copy-start.2 = (f32[2,3,3,128]{3,0,2,1:T(2,128)S(1)}, f32[2,3,3,128]{3,0,2,1:T(2,128)}, u32[]{:S(2)}) copy-start(f32[2,3,3,128]{3,0,2,1:T(2,128)} %param.14) | copy-start | bytes 27652
  0.7 31.4 %copy-start.6 = (s32[128]{0:T(128)S(1)}, s32[128]{0:T(128)}, u32[]{:S(2)}) copy-start(s32[128]{0:T(128)} %param.15) | copy-start | bytes 1540
  4.5 4.6 %collective-permute-start = (bf16[16,80,128]{2,1,0:T(8,128)(2,1)S(1)}, bf16[16,80,128]{2,1,0:T(8,128)(2,1)S(1)}, u32[]{:S(2)}, u32[]{:S(2)}) collective-permute-start(bf16[16,80,128]{2,1,0:T(8,128)(2,1)S(1)} %get-tuple-element.18), channel_id=1, source_target_pairs={{0,1},{1,0},{2,3},{3,2},{4,5},{5,4},{6,7},{7,6},{8,9},{9,8},{10,11... | collective-permute-start | bytes 983048 | tf_op jit(solution)/shard_map/ppermute | solution.py:350
  32.5 2.8 %collective-permute-start.1 = (bf16[16,2,384]{2,1,0:T(2,128)(2,1)S(1)}, bf16[16,2,384]{2,1,0:T(2,128)(2,1)S(1)}, u32[]{:S(2)}, u32[]{:S(2)}) collective-permute-start(bf16[16,2,384]{2,1,0:T(2,128)(2,1)S(1)} %get-tuple-element.25), channel_id=1, source_target_pairs={{0,1},{1,0},{2,3},{3,2},{4,5},{5,4},{6,7},{7,6},{8,9},{9,8},{10,11... | collective-permute-start | bytes 73736 | tf_op jit(solution)/shard_map/ppermute | solution.py:399

commit v7 on v6

--- a/solution.py
+++ b/solution.py
@@ -15,8 +15,7 @@
 
 
 def slot_of(chip, chips):
-    half = chips // 2
-    return lax.rem(chip, half) * 2 + lax.div(chip, half)
+    return lax.rem(lax.rem(chip, 8) * 5, 8) * 2 + lax.div(chip, 8)
 
 
 def alternate(order):
@@ -375,7 +374,7 @@
         compiler_params=grant(8),
         name="add_pair",
     )(own, swapped, free)
-    same_core = [[2 * t + c for t in alternate(range(chips // 2))] for c in range(2)]
+    same_core = [[2 * t + c for t in alternate([5 * i % 8 for i in range(8)])] for c in range(2)]
     arrived = lax.all_to_all(
         paired, "hist", split_axis=0, concat_axis=0, tiled=True, axis_index_groups=same_core
     )

time: 54.7 us -> 54.7 us (level)
  blocking collectives: 40.4 us -> 39.3 us
  starting transfers between devices: 5.23 us -> 6.26 us
    all_to_all x1, blocking collectives: 22.8 us -> 21.4 us  [per_device(): lax.all_to_all(paired, 'hist', split_axis=0, concat_axis=0, tiled=True, a...]
    ppermute x2, starting transfers between devices: 5.23 us -> 6.26 us  [per_device(): swapped = lax.ppermute(other, 'hist', cores)]
where the time goes in v7:
time: 54.7 us; the launch traced here: 53.7 us
  blocking collectives  39.3 us (72%)
  starting transfers between devices  6.26 us (11%)
  Pallas kernels  5.54 us (10%)
  between operations  1.43 us (3%)
  waiting for transfers between devices  1.13 us (2%)
    all_to_all x1, blocking collectives, per_device(): lax.all_to_all(paired, 'hist', split_axis=0, concat_axis=0, tiled=True, a...  21.4 us
    all_to_all x1, blocking collectives, per_device(): lax.all_to_all(paired.reshape(ka_size * chips, 2, 3 * lanes), ('ka', 'his...  18 us
    ppermute x2, starting transfers between devices, per_device(): swapped = lax.ppermute(other, 'hist', cores)  6.26 us
    pallas_call x1, Pallas kernels, per_device(): pl.pallas_call(terms_kernel, out_shape=(tiles, tiles, jax.ShapeDtypeStruc...  3.13 us
    ppermute x2, waiting for transfers between devices, per_device(): swapped = lax.ppermute(other, 'hist', cores)  1.13 us
  transfers between devices with their start and end apart: 2, of which 2 were waited for; matrix products, arithmetic and copies ran while one was open for 0% of the time, Pallas kernels for 2%

profile of v7, /device:TPU:1, one launch (start us, length us, event | category | flops | bytes accessed | tf_op | source)
XLA Modules:
  0.0 53.7 jit_solution(17978904400732397109)
XLA Ops:
  0.6 0.0 copy-start.1
  0.6 0.0 copy-start.3
  0.7 0.0 copy-start
  0.7 0.0 copy-start.4
  0.7 0.0 copy-start.5
  0.7 0.0 copy-start.2
  0.7 0.0 copy-start.6
  1.4 3.1 %terms.1 = (bf16[16,80,128]{2,1,0:T(8,128)(2,1)S(1)}, bf16[16,80,128]{2,1,0:T(8,128)(2,1)S(1)}, s32[1,128]{1,0:T(1,128)S(1)}) custom-call(s32[1]{0:T(128)S(6)} %copy.13.step, bf16[4,3,3,2,128]{4,3,2,1,0:T(2,128)(2,1)} %bitcast.19, f32[3,4,128]{2,1,0:T(4,128)} %bitcast.12, bf16[4,2,3,3,128,128]{5,4,3,2,1,0:T(8,128)(2,1)} %history.1), custom_call_target="tpu_custom_call" | custom-call | tf_op jit(solution)/shard_map/terms/pallas_call | solution.py:333
  4.6 3.3 %collective-permute-start = (bf16[16,80,128]{2,1,0:T(8,128)(2,1)S(1)}, bf16[16,80,128]{2,1,0:T(8,128)(2,1)S(1)}, u32[]{:S(2)}, u32[]{:S(2)}) collective-permute-start(bf16[16,80,128]{2,1,0:T(8,128)(2,1)S(1)} %get-tuple-element.18), channel_id=1, source_target_pairs={{0,1},{1,0},{2,3},{3,2},{4,5},{5,4},{6,7},{7,6},{8,9},{9,8},{10,11... | collective-permute-start | bytes 983048 | tf_op jit(solution)/shard_map/ppermute | solution.py:349
  7.9 0.0 copy-done.3
  7.9 0.0 copy-done
  7.9 0.0 copy-done.4
  7.9 0.3 ahead.1
  8.2 0.9 %collective-permute-done.arrived = bf16[16,80,128]{2,1,0:T(8,128)(2,1)S(1)} collective-permute-done((bf16[16,80,128]{2,1,0:T(8,128)(2,1)S(1)}, bf16[16,80,128]{2,1,0:T(8,128)(2,1)S(1)}, u32[]{:S(2)}, u32[]{:S(2)}) %collective-permute-start) | collective-permute-done | bytes 327712 | tf_op jit(solution)/shard_map/ppermute | solution.py:349
  9.1 0.1 add_pair.1
  9.3 21.4 %all_to_all.10.arrived = bf16[16,80,128]{2,1,0:T(8,128)(2,1)S(1)} all-to-all(bf16[16,80,128]{2,1,0:T(8,128)(2,1)S(1)} %add_pair.1), channel_id=1, replica_groups={{0,16,10,26,4,20,14,30,8,24,2,18,12,28,6,22},{1,17,11,27,5,21,15,31,9,2..., dimensions={0} | all-to-all | bytes 655360 | tf_op jit(solution)/shard_map/all_to_all | solution.py:378
  30.6 0.0 copy-done.6
  30.6 0.4 rows.1
  31.0 2.9 %collective-permute-start.1 = (bf16[16,2,384]{2,1,0:T(2,128)(2,1)S(1)}, bf16[16,2,384]{2,1,0:T(2,128)(2,1)S(1)}, u32[]{:S(2)}, u32[]{:S(2)}) collective-permute-start(bf16[16,2,384]{2,1,0:T(2,128)(2,1)S(1)} %get-tuple-element.25), channel_id=1, source_target_pairs={{0,1},{1,0},{2,3},{3,2},{4,5},{5,4},{6,7},{7,6},{8,9},{9,8},{10,11... | collective-permute-start | bytes 73736 | tf_op jit(solution)/shard_map/ppermute | solution.py:398
  34.0 0.6 %lattice.1 = (bf16[4,3,3,2,128]{4,3,2,1,0:T(2,128)(2,1)}, f32[1,128]{1,0:T(1,128)S(1)}) custom-call(f32[18,4,128]{2,1,0:T(4,128)S(1)} %get-tuple-element.22.fresh), custom_call_target="tpu_custom_call" | custom-call | flops 10000 | bytes 60000 | tf_op jit(solution)/shard_map/lattice/pallas_call | solution.py:399
  34.6 0.2 collective-permute-done.1.arrived
  34.8 0.1 add_shares.1
  34.9 18.0 %all_to_all.11.got = bf16[128,2,384]{2,1,0:T(2,128)(2,1)S(1)} all-to-all(bf16[128,2,384]{2,1,0:T(2,128)(2,1)S(1)} %bitcast.11), channel_id=1, replica_groups={{0,128,32,160,64,192,96,224,16,144,48,176,80,208,112,240,8,136,40,168,7..., dimensions={0} | all-to-all | bytes 393216 | tf_op jit(solution)/shard_map/all_to_all | solution.py:423
  52.8 0.9 %finish.1 = (f32[3,3,2,4]{3,2,1,0:T(2,128)}, f32[2,4,64]{2,1,0:T(4,128)}) custom-call(bf16[128,2,384]{2,1,0:T(2,128)(2,1)S(1)} %all_to_all.11.got, f32[4,128]{1,0:T(4,128)S(1)} %get-tuple-element.19._.free), custom_call_target="tpu_custom_call" | custom-call | tf_op jit(solution)/shard_map/finish/pallas_call | solution.py:431
  (3 shorter events, 0.0 us)
Async XLA Ops:
  0.6 30.0 %copy-start.1 = (f32[4,3,128]{2,0,1:T(4,128)S(1)}, f32[4,3,128]{2,0,1:T(4,128)}, u32[]{:S(2)}) copy-start(f32[4,3,128]{2,0,1:T(4,128)} %param.11) | copy-start | bytes 18436
  0.6 7.2 %copy-start.3 = (f32[2,64,4]{1,2,0:T(4,128)S(1)}, f32[2,64,4]{1,2,0:T(4,128)}, u32[]{:S(2)}) copy-start(f32[2,64,4]{1,2,0:T(4,128)} %param.18) | copy-start | bytes 6148
  0.7 7.2 %copy-start = (bf16[4,2,64,128]{3,2,1,0:T(8,128)(2,1)S(1)}, bf16[4,2,64,128]{3,2,1,0:T(8,128)(2,1)}, u32[]{:S(2)}) copy-start(bf16[4,2,64,128]{3,2,1,0:T(8,128)(2,1)} %pseudo.1) | copy-start | bytes 393220
  0.7 7.2 %copy-start.4 = (s32[64,6]{0,1:T(8,128)S(1)}, s32[64,6]{0,1:T(8,128)}, u32[]{:S(2)}) copy-start(s32[64,6]{0,1:T(8,128)} %param.17) | copy-start | bytes 4612
  0.7 7.2 %copy-start.5 = (f32[64]{0:T(128)S(1)}, f32[64]{0:T(128)}, u32[]{:S(2)}) copy-start(f32[64]{0:T(128)} %param.16) | copy-start | bytes 772
  0.7 30.0 %copy-start.2 = (f32[2,3,3,128]{3,0,2,1:T(2,128)S(1)}, f32[2,3,3,128]{3,0,2,1:T(2,128)}, u32[]{:S(2)}) copy-start(f32[2,3,3,128]{3,0,2,1:T(2,128)} %param.14) | copy-start | bytes 27652
  0.7 29.9 %copy-start.6 = (s32[128]{0:T(128)S(1)}, s32[128]{0:T(128)}, u32[]{:S(2)}) copy-start(s32[128]{0:T(128)} %param.15) | copy-start | bytes 1540
  4.6 4.6 %collective-permute-start = (bf16[16,80,128]{2,1,0:T(8,128)(2,1)S(1)}, bf16[16,80,128]{2,1,0:T(8,128)(2,1)S(1)}, u32[]{:S(2)}, u32[]{:S(2)}) collective-permute-start(bf16[16,80,128]{2,1,0:T(8,128)(2,1)S(1)} %get-tuple-element.18), channel_id=1, source_target_pairs={{0,1},{1,0},{2,3},{3,2},{4,5},{5,4},{6,7},{7,6},{8,9},{9,8},{10,11... | collective-permute-start | bytes 983048 | tf_op jit(solution)/shard_map/ppermute | solution.py:349
  31.0 3.8 %collective-permute-start.1 = (bf16[16,2,384]{2,1,0:T(2,128)(2,1)S(1)}, bf16[16,2,384]{2,1,0:T(2,128)(2,1)S(1)}, u32[]{:S(2)}, u32[]{:S(2)}) collective-permute-start(bf16[16,2,384]{2,1,0:T(2,128)(2,1)S(1)} %get-tuple-element.25), channel_id=1, source_target_pairs={{0,1},{1,0},{2,3},{3,2},{4,5},{5,4},{6,7},{7,6},{8,9},{9,8},{10,11... | collective-permute-start | bytes 73736 | tf_op jit(solution)/shard_map/ppermute | solution.py:398
